TPU v7x, 32 devices: a whole 2x2x4 slice. The times are simulated.
32 devices in a mesh: groups: 2 (over y), dap: 4 (over z), branch: 2 (over x), chan: 2 (over core).
Axes of the slice: x: 2, y: 2, z: 4, core: 2. Of those that a mesh axis runs over, the one named last changes fastest.
Arguments:
- homolog_features: bfloat16 [128, 128, 256], P(('groups', 'dap', 'branch', 'chan')), parts along dimension 0, may hold values from -0.14941406 to 0.14941406
- alignment_tokens: int32 [128, 128], P(('groups', 'dap', 'branch', 'chan')), parts along dimension 0, may hold values from 0 to 22
- alignment_mask: int32 [128, 128], P(('groups', 'dap', 'branch', 'chan')), parts along dimension 0, may hold values 0 or 1
- pair_activation_input: bfloat16 [256, 128, 128], P(('groups', 'dap'), ('branch', 'chan')), parts along dimension 0, may hold values from -6 to 6
- pair_residue_mask: int32 [256, 128], P(('groups', 'dap'), ('branch', 'chan')), parts along dimension 0, may hold values 0 or 1
- letter_lookup_matrix: bfloat16 [23, 256], replicated, may hold values from -0.14941406 to 0.14941406
- homolog_focus_scaling: float32 [256], replicated, may hold values from 0.5 to 1.5
- focus_entry_matrix: bfloat16 [256, 1024], replicated, may hold values from -0.375 to 0.375
- focus_exit_matrix: bfloat16 [256, 256], replicated, may hold values from -0.375 to 0.375
- pair_norm_gain: float32 [128], replicated, may hold values from 0.5 to 1.5
- head_bias_weight: bfloat16 [128, 8], replicated, may hold values from -40 to 40
- tensor_product_scaling: float32 [256], replicated, may hold values from 0.5 to 1.5
- tensor_product_matrix: bfloat16 [256, 64], replicated, may hold values from -0.375 to 0.375
- outer_output_weight: bfloat16 [1024, 128], replicated, may hold values from -1.5 to 1.5
- triangle_input_weight: bfloat16 [128, 640], replicated, may hold values from -0.5 to 0.5
- triangle_norm_gain: float32 [128], replicated, may hold values from 0.5 to 1.5
- triangle_output_weight: bfloat16 [128, 128], replicated, may hold values from -0.5 to 0.5
Outputs:
- alignment_output: bfloat16 [128, 128, 256], P(('groups', 'dap', 'branch', 'chan')), parts along dimension 0
- pair_activation_output: bfloat16 [256, 128, 128], P(('groups', 'dap'), ('branch', 'chan')), parts along dimension 0
There are 2 independent parts, one for each index of `groups`. A program takes and returns all parts, laid end to end along the dimension named above; an argument that names none is the same for every part. Nothing has to cross between parts.
All inputs are finite; a program needn't handle non-finite values. No bound on the sum of `alignment_mask` or of `pair_residue_mask` on one device may be relied on, other than what follows from the above.
Results may differ from a plain program's by a relative error of at most 0.011.
The roundings to bfloat16 on the way count: a program that leaves them out, or rounds other values in their place, can miss the bound.
Values may be sent and summed in bfloat16 or wider, within the bound.
A program may use at most 128 MiB of HBM per device.

v0:
```python
import functools

import jax
import jax.numpy as jnp
from jax import lax
from jax.experimental import pallas as pl
from jax.experimental.pallas import tpu as pltpu
from jax.sharding import PartitionSpec as P


def layer_normalize(values, gain_vector, norm_axis):
    center = values - jnp.mean(values, axis=norm_axis, keepdims=True)
    spread = jnp.mean(center * center, axis=norm_axis, keepdims=True)
    return center * lax.rsqrt(spread + 1e-05) * gain_vector


def channel_products(left_part, right_part, dap_count, column_count, rows_block, column_block):
    row_ratio = dap_count // column_count
    channels_here = left_part.size // (dap_count * column_count * rows_block * column_block)
    left_five = left_part.reshape(dap_count, column_count, channels_here, rows_block, column_block)
    right_six = right_part.reshape(
        column_count, row_ratio, column_count, channels_here, rows_block, column_block
    )
    product = jnp.einsum(
        "pqrik,bhqrjk->pbrihj", left_five, right_six, preferred_element_type=jnp.float32
    )
    return product.astype(jnp.bfloat16)


def shards(
    homolog_features,
    alignment_tokens,
    alignment_mask,
    pair_activation_input,
    pair_residue_mask,
    letter_lookup_matrix,
    homolog_focus_scaling,
    focus_entry_matrix,
    focus_exit_matrix,
    pair_norm_gain,
    head_bias_weight,
    tensor_product_scaling,
    tensor_product_matrix,
    outer_output_weight,
    triangle_input_weight,
    triangle_norm_gain,
    triangle_output_weight,
):
    dap_count = lax.axis_size("dap")
    column_count = lax.axis_size("branch") * lax.axis_size("chan")
    device_count = dap_count * column_count
    rows_block, column_block, pair_width = pair_activation_input.shape
    sequence_total, residue_total, alignment_width = homolog_features.shape
    number_heads = head_bias_weight.shape[1]
    per_head_width = alignment_width // number_heads
    outer_factor_width = tensor_product_matrix.shape[1] // 2
    pair_normed = layer_normalize(
        pair_activation_input.astype(jnp.float32), pair_norm_gain, -1
    ).astype(jnp.bfloat16)
    bias_block = jnp.einsum(
        "ikc,ch->hik", pair_normed, head_bias_weight, preferred_element_type=jnp.float32
    )
    tri_linear = jnp.einsum(
        "ikc,ce->eik",
        pair_normed,
        triangle_input_weight[:, : 4 * pair_width],
        preferred_element_type=jnp.float32,
    )
    mask_pair = pair_residue_mask.astype(jnp.float32)
    tri_left = (
        jax.nn.sigmoid(tri_linear[pair_width : 2 * pair_width])
        * tri_linear[:pair_width]
        * mask_pair
    ).astype(jnp.bfloat16)
    tri_right = (
        jax.nn.sigmoid(tri_linear[3 * pair_width : 4 * pair_width])
        * tri_linear[2 * pair_width : 3 * pair_width]
        * mask_pair
    ).astype(jnp.bfloat16)
    out_gate = jnp.einsum(
        "ikc,ce->ike",
        pair_normed,
        triangle_input_weight[:, 4 * pair_width :],
        preferred_element_type=jnp.float32,
    )
    per_device = pair_width // device_count
    flat_shape = (device_count, 1, per_device, rows_block, column_block)
    products = channel_products(
        lax.all_to_all(
            tri_left.reshape(flat_shape),
            ("dap", "branch", "chan"),
            split_axis=0,
            concat_axis=1,
            tiled=True,
        ),
        lax.all_to_all(
            tri_right.reshape(flat_shape),
            ("dap", "branch", "chan"),
            split_axis=0,
            concat_axis=1,
            tiled=True,
        ),
        dap_count,
        column_count,
        rows_block,
        column_block,
    )
    channels_here = products.shape[2]
    sending = products.reshape(device_count, 1, channels_here, rows_block, column_block)
    returned = lax.all_to_all(
        sending, ("dap", "branch", "chan"), split_axis=0, concat_axis=1, tiled=True
    )
    tri_sum = returned.reshape(pair_width, rows_block, column_block)
    tri_normed = layer_normalize(
        tri_sum.astype(jnp.float32), triangle_norm_gain[:, None, None], 0
    ).astype(jnp.bfloat16)
    tri_update = jax.nn.sigmoid(out_gate) * jnp.einsum(
        "cik,ce->ike", tri_normed, triangle_output_weight, preferred_element_type=jnp.float32
    )
    token_class_count = letter_lookup_matrix.shape[0]
    token_indicator = (
        alignment_tokens[:, :, None] == jnp.arange(token_class_count, dtype=jnp.int32)
    ).astype(jnp.bfloat16)
    embedded_tokens = homolog_features.astype(jnp.float32) + jnp.einsum(
        "snv,vc->snc", token_indicator, letter_lookup_matrix, preferred_element_type=jnp.float32
    )
    alignment_normalized = layer_normalize(embedded_tokens, homolog_focus_scaling, -1).astype(
        jnp.bfloat16
    )
    projected_values = jnp.einsum(
        "rdz,zg->rdg", alignment_normalized, focus_entry_matrix, preferred_element_type=jnp.float32
    )
    query_rows = projected_values[:, :, :alignment_width].astype(jnp.bfloat16)
    every_key = projected_values[:, :, alignment_width : 2 * alignment_width].astype(jnp.bfloat16)
    every_value = projected_values[:, :, 2 * alignment_width : 3 * alignment_width].astype(
        jnp.bfloat16
    )
    gate_values = projected_values[:, :, 3 * alignment_width :]
    key_mask_bias = (alignment_mask.astype(jnp.float32) - 1.0) * 1000000000.0
    score_scale = per_head_width ** (-0.5)
    bias_partial = lax.all_gather(bias_block, ("branch", "chan"), axis=2, tiled=True)
    bias_full = lax.all_gather(bias_partial, "dap", axis=1, tiled=True)
    query_form = query_rows.reshape(sequence_total, residue_total, number_heads, per_head_width)
    key_form = every_key.reshape(sequence_total, residue_total, number_heads, per_head_width)
    value_form = every_value.reshape(sequence_total, residue_total, number_heads, per_head_width)
    mask_form = key_mask_bias.reshape(sequence_total, 1, 1, residue_total)

    def attend(seq_item):
        query_seq, key_seq, value_seq, mask_seq = seq_item
        scores = (
            jnp.einsum("ihd,jhd->hij", query_seq, key_seq, preferred_element_type=jnp.float32)
            * score_scale
            + bias_full
            + mask_seq
        )
        largest = jnp.max(scores, axis=2, keepdims=True)
        exponent = jnp.exp(scores - largest)
        attention_weights = (exponent / jnp.sum(exponent, axis=2, keepdims=True)).astype(
            jnp.bfloat16
        )
        return jnp.einsum(
            "bqo,obm->qbm", attention_weights, value_seq, preferred_element_type=jnp.float32
        )

    attended_rows = lax.map(attend, (query_form, key_form, value_form, mask_form)).reshape(
        sequence_total, residue_total, alignment_width
    )
    gated_output = (attended_rows * jax.nn.sigmoid(gate_values)).astype(jnp.bfloat16)
    alignment_output = (
        embedded_tokens
        + jnp.einsum(
            "rdz,zg->rdg", gated_output, focus_exit_matrix, preferred_element_type=jnp.float32
        )
    ).astype(jnp.bfloat16)
    outer_normalized = layer_normalize(
        alignment_output.astype(jnp.float32), tensor_product_scaling, -1
    ).astype(jnp.bfloat16)
    alignment_mask_rows = alignment_mask.astype(jnp.float32)[:, :, None]
    left_projection = (
        (
            jnp.einsum(
                "rdz,zg->rdg",
                outer_normalized,
                tensor_product_matrix[:, :outer_factor_width],
                preferred_element_type=jnp.float32,
            )
            * alignment_mask_rows
        )
        .astype(jnp.bfloat16)
        .reshape(sequence_total, residue_total * outer_factor_width)
    )
    right_projection = (
        (
            jnp.einsum(
                "rdz,zg->rdg",
                outer_normalized,
                tensor_product_matrix[:, outer_factor_width:],
                preferred_element_type=jnp.float32,
            )
            * alignment_mask_rows
        )
        .astype(jnp.bfloat16)
        .reshape(sequence_total, residue_total * outer_factor_width)
    )
    left_gathered, right_gathered = (
        lax.all_gather(left_projection, ("branch", "chan"), axis=0, tiled=True),
        lax.all_gather(right_projection, ("branch", "chan"), axis=0, tiled=True),
    )
    column_index = lax.axis_index("branch") * lax.axis_size("chan") + lax.axis_index("chan")
    right_block = lax.dynamic_slice_in_dim(
        right_gathered,
        column_index * (column_block * outer_factor_width),
        column_block * outer_factor_width,
        1,
    )
    left_block = lax.all_to_all(left_gathered, "dap", split_axis=1, concat_axis=0, tiled=True)
    right_full = lax.all_gather(right_block, "dap", axis=0, tiled=True)
    total_seqs = left_block.shape[0]
    outer = jnp.einsum(
        "sic,sjd->ijcd",
        left_block.reshape(total_seqs, rows_block, outer_factor_width),
        right_full.reshape(total_seqs, column_block, outer_factor_width),
        preferred_element_type=jnp.float32,
    ) * (1.0 / total_seqs)
    flat_outer = outer.astype(jnp.bfloat16).reshape(
        rows_block * column_block, outer_factor_width * outer_factor_width
    )
    outer_update = jnp.dot(
        flat_outer, outer_output_weight, preferred_element_type=jnp.float32
    ).reshape(rows_block, column_block, pair_width)
    pair_activation_output = (
        pair_activation_input.astype(jnp.float32) + tri_update + outer_update
    ).astype(jnp.bfloat16)
    return (alignment_output, pair_activation_output)


LANES = 128
SUB = 8


def dot_nn(left, right):
    return lax.dot_general(left, right, (((1,), (0,)), ((), ())), preferred_element_type=jnp.float32)


def dot_nt(left, right):
    return lax.dot_general(left, right, (((1,), (1,)), ((), ())), preferred_element_type=jnp.float32)


def chunk_swap(parts, width):
    parts = list(parts)
    lane = lax.broadcasted_iota(jnp.int32, parts[0].shape, parts[0].ndim - 1)
    axis = parts[0].ndim - 1
    step = len(parts) // 2
    while step >= 1:
        span = step * width
        low = (lane // span) % 2 == 0
        for a in range(len(parts)):
            if (a // step) % 2 == 0:
                lo, hi = parts[a], parts[a + step]
                parts[a] = jnp.where(low, lo, pltpu.roll(hi, span, axis))
                parts[a + step] = jnp.where(low, pltpu.roll(lo, LANES - span, axis), hi)
        step //= 2
    return parts


def norm_rows(values, gain):
    center = values - jnp.mean(values, axis=-1, keepdims=True)
    spread = jnp.mean(center * center, axis=-1, keepdims=True)
    return center * lax.rsqrt(spread + 1e-05) * gain


def staged_kernel(sizes, order, *refs):
    count = len(order)
    sources, rest = refs[:count], refs[count : len(refs) - count - 1]
    held, sems = refs[len(refs) - count - 1 : -1], refs[-1]
    fetches = [pltpu.make_async_copy(sources[i], held[i], sems.at[i]) for i in range(count)]

    def begin():
        for i in order:
            fetches[i].start()

    def ready(*which):
        for i in which:
            fetches[i].wait()

    block_kernel(sizes, begin, ready, *held, *rest)


def block_kernel(
    sizes,
    begin,
    ready,
    feat,
    tokens,
    amask,
    pair,
    pmask,
    table,
    focus_gain,
    entry,
    exit_w,
    pair_gain,
    head_t,
    product_gain,
    prod_t,
    outer_w,
    tri_w,
    tri_gain,
    tri_out,
    align_out,
    pair_out,
    pn,
    bsend,
    brecv,
    tsend,
    trecv,
    lsend,
    rsend,
    lrecv,
    rrecv,
    zsend,
    zrecv,
    stage_a,
    stage_b,
    bias_full,
    emb,
    qm,
    kv,
    gates,
    normed,
    w2t,
    upd,
    table_f,
    left_w,
    gate_f,
    b_send,
    b_recv,
    t_send,
    t_recv,
    o_send,
    o_recv,
    z_send,
    z_recv,
    l_send,
    l_recv,
):
    P_, B_, K_ = sizes
    Q_ = B_ * K_
    D_ = P_ * Q_
    rows, cols, cz = pair.shape
    seqs, res, width = feat.shape
    heads = head_t.shape[0]
    hw = width // heads
    per = LANES // hw
    groups = width // LANES
    fac = prod_t.shape[0] // 2
    nch = LANES // cols
    G = rows // nch
    mp = lax.axis_index("dap")
    mq = lax.axis_index("branch") * K_ + lax.axis_index("chan")
    me = mp * Q_ + mq

    def where_is(p, q):
        return {"dap": p, "branch": q // K_, "chan": q % K_}

    def peer(off):
        n = lax.rem(me + off, D_)
        return n, where_is(n // Q_, n % Q_)

    def remote(src, dst, ss, rs, dev):
        return pltpu.make_async_remote_copy(
            src_ref=src,
            dst_ref=dst,
            send_sem=ss,
            recv_sem=rs,
            device_id=dev,
            device_id_type=pl.DeviceIdType.MESH,
        )

    def exchange(send, recv, ss, rs):
        copies = []
        for off in range(1, D_):
            n, dev = peer(off)
            c = remote(send(n), recv.at[me], ss.at[off], rs.at[off], dev)
            c.start()
            copies.append(c)
        return copies

    def spread(send, recv, ss, rs):
        copies = []
        for op in range(1, P_):
            p = lax.rem(mp + op, P_)
            copies.append(
                remote(send(p), recv.at[me], ss.at[op * Q_], rs.at[op * Q_], where_is(p, mq))
            )
        for oq in range(1, Q_):
            dev = where_is(mp, lax.rem(mq + oq, Q_))
            copies.append(remote(send(mp), recv.at[me], ss.at[oq], rs.at[oq], dev))
        for c in copies:
            c.start()
        return copies

    def forward(copies, recv, ss, rs):
        for op in range(1, P_):
            copies[op - 1].wait_recv()
            src = lax.rem(mp + P_ - op, P_) * Q_ + mq
            for oq in range(1, Q_):
                c = remote(
                    recv.at[src],
                    recv.at[src],
                    ss.at[op * Q_ + oq],
                    rs.at[op * Q_ + oq],
                    where_is(mp, lax.rem(mq + oq, Q_)),
                )
                c.start()
                copies.append(c)

    barrier = pltpu.get_barrier_semaphore()
    for off in range(1, D_):
        pl.semaphore_signal(
            barrier, inc=1, device_id=peer(off)[1], device_id_type=pl.DeviceIdType.MESH
        )

    begin()
    ready(3, 9)
    pair_f = pair[...].astype(jnp.float32).reshape(rows * cols, cz)
    pn[...] = norm_rows(pair_f, pair_gain[...]).astype(jnp.bfloat16)

    def pair_rows(g):
        return jnp.concatenate(
            [pn[(a * G + g) * cols : (a * G + g + 1) * cols, :] for a in range(nch)], axis=0
        )

    ready(10)
    for g in range(G):
        bsend[g * heads : (g + 1) * heads, :] = dot_nt(head_t[...], pair_rows(g))
    brecv[me] = bsend[...]
    pl.semaphore_wait(barrier, D_ - 1)
    bias_copies = spread(lambda p: bsend, brecv, b_send, b_recv)

    per_dev = cz // D_
    unit = G * per_dev
    ready(4, 14)
    mrows = jnp.concatenate(
        [pmask[a * G : (a + 1) * G, :].astype(jnp.float32) for a in range(nch)], axis=1
    )
    tri_copies = []
    for side in range(2):
        at = 2 * side * cz
        tri_t = tri_w[:, at : at + 2 * cz].astype(jnp.float32).T.astype(jnp.bfloat16)
        for t in range(G // 2):
            block = jnp.concatenate([pair_rows(2 * t), pair_rows(2 * t + 1)], axis=0)
            lin = dot_nt(tri_t, block)
            mrow = jnp.concatenate([mrows[2 * t : 2 * t + 1], mrows[2 * t + 1 : 2 * t + 2]], axis=1)
            val = jax.nn.sigmoid(lin[cz:]) * lin[:cz] * mrow
            for n in range(D_):
                piece = val[n * per_dev : (n + 1) * per_dev]
                two = jnp.concatenate([piece[:, :LANES], piece[:, LANES:]], axis=0)
                tsend[side, n, 2 * t * per_dev : 2 * (t + 1) * per_dev, :] = two.astype(
                    jnp.bfloat16
                )
        trecv[side, me] = tsend[side, me]
        tri_copies.append(
            exchange(
                lambda n: tsend.at[side, n], trecv.at[side], t_send.at[side], t_recv.at[side]
            )
        )

    forward(bias_copies, brecv, b_send, b_recv)

    ready(0, 1, 2, 5, 6, 7, 8, 11, 12, 13, 15, 16)
    table_f[...] = jnp.zeros_like(table_f)
    table_f[: table.shape[0], :] = table[...].astype(jnp.float32)
    table_all = table_f[...].astype(jnp.bfloat16)
    four = jnp.concatenate([prod_t[:fac, :].astype(jnp.float32)] * nch, axis=0).T
    lane_fac = lax.broadcasted_iota(jnp.int32, four.shape, 1) // fac
    for a in range(nch):
        left_w[a * width : (a + 1) * width, :] = jnp.where(lane_fac == a, four, 0.0).astype(
            jnp.bfloat16
        )
    lane_head = lax.broadcasted_iota(jnp.int32, (res, LANES), 1) // hw
    for s in range(seqs):
        kinds = lax.broadcasted_iota(jnp.int32, (LANES, res), 0)
        hot = jnp.where(kinds == tokens[s : s + 1, :], 1.0, 0.0).astype(jnp.float32)
        here = feat[s].astype(jnp.float32) + dot_nn(hot.T.astype(jnp.bfloat16), table_all)
        emb[s] = here
        proj = dot_nn(norm_rows(here, focus_gain[...]).astype(jnp.bfloat16), entry[...])
        for b in range(groups):
            qb = proj[:, b * LANES : (b + 1) * LANES]
            for h in range(per):
                qm[s, b, h * res : (h + 1) * res, :] = jnp.where(
                    lane_head == h, qb, 0.0
                ).astype(jnp.bfloat16)
        kv[s] = proj[:, width : 3 * width].astype(jnp.bfloat16)
        gates[s] = jax.nn.sigmoid(proj[:, 3 * width :])

    stage_a[...] = outer_w[...].astype(jnp.float32)
    for g in range(SUB):
        piece = jnp.concatenate(
            [stage_a[pl.ds(a * SUB + g, fac, stride=fac), :] for a in range(fac // SUB)], axis=0
        )
        w2t[:, g * LANES : (g + 1) * LANES] = piece.T.astype(jnp.bfloat16)

    for c in bias_copies[P_ - 1 :]:
        c.wait_recv()
    for p in range(P_):
        got = chunk_swap([brecv[p * Q_ + q] for q in range(Q_)], cols)
        for a in range(nch):
            stage_a[(p * nch + a) * G * heads : (p * nch + a + 1) * G * heads, :] = got[a]
    for h in range(heads):
        bias_full[h * res : (h + 1) * res, :] = stage_a[pl.ds(h, res, stride=heads), :]

    scale = hw ** (-0.5)
    for s in range(seqs):
        mask_row = (amask[s : s + 1, :].astype(jnp.float32) - 1.0) * 1000000000.0
        gated = []
        for b in range(groups):
            key = kv[s, :, b * LANES : (b + 1) * LANES]
            val = kv[s, :, width + b * LANES : width + (b + 1) * LANES]
            sc = dot_nt(qm[s, b], key) * scale
            sc = sc + bias_full[b * per * res : (b + 1) * per * res, :] + mask_row
            ex = jnp.exp(sc - jnp.max(sc, axis=1, keepdims=True))
            wt = (ex / jnp.sum(ex, axis=1, keepdims=True)).astype(jnp.bfloat16)
            av = dot_nn(wt, val)
            att = av[:res]
            for h in range(1, per):
                att = jnp.where(lane_head == h, av[h * res : (h + 1) * res], att)
            gated.append((att * gates[s, :, b * LANES : (b + 1) * LANES]).astype(jnp.bfloat16))
        out = (emb[s] + dot_nn(jnp.concatenate(gated, axis=1), exit_w[...])).astype(jnp.bfloat16)
        align_out[s] = out
        on = norm_rows(out.astype(jnp.float32), product_gain[...])
        on = on.astype(jnp.bfloat16).astype(jnp.float32)
        mcol = jnp.broadcast_to(amask[s : s + 1, :].astype(jnp.float32), (res, res)).T
        normed[s * res : (s + 1) * res, :] = on * jnp.concatenate([mcol] * groups, axis=1)

    wide = []
    for a in range(nch):
        wide.append(
            jnp.concatenate(
                [
                    normed[s * res + p * rows + a * G : s * res + p * rows + (a + 1) * G, :]
                    for s in range(seqs)
                    for p in range(P_)
                ],
                axis=0,
            ).astype(jnp.bfloat16)
        )
    left = dot_nn(jnp.concatenate(wide, axis=1), left_w[...])
    right = dot_nt(prod_t[fac:, :], normed[...].astype(jnp.bfloat16))
    lefts = [
        jnp.concatenate(
            [left[(s * P_ + p) * G : (s * P_ + p + 1) * G] for s in range(seqs)], axis=0
        ).astype(jnp.bfloat16)
        for p in range(P_)
    ]
    by_seq = []
    for s in range(seqs):
        by_seq.append(
            chunk_swap(
                [right[a * SUB : (a + 1) * SUB, s * res : (s + 1) * res] for a in range(nch)], cols
            )
        )
    half = seqs * SUB
    for p in range(P_):
        lsend[p] = lefts[p]
    for q in range(Q_):
        rsend[q] = jnp.concatenate([by_seq[s][q] for s in range(seqs)], axis=0).astype(jnp.bfloat16)
    lrecv[me] = lsend[mp]
    rrecv[me] = rsend[mq]
    left_copies = spread(lambda p: lsend.at[p], lrecv, l_send, l_recv)
    right_copies = exchange(lambda n: rsend.at[n % Q_], rrecv, o_send, o_recv)

    for g in range(G):
        gate_f[g] = jax.nn.sigmoid(dot_nn(pair_rows(g), tri_w[:, 4 * cz :]))

    for side, stage in enumerate((stage_a, stage_b)):
        for c in tri_copies[side]:
            c.wait_recv()
        for p in range(P_):
            got = chunk_swap(
                [
                    trecv[side, p * Q_ + q].astype(jnp.float32)
                    for q in range(Q_)
                ],
                cols,
            )
            for a in range(nch):
                stage[(p * nch + a) * unit : (p * nch + a + 1) * unit, :] = got[a]
    sums = []
    for c in range(per_dev):
        lc = stage_a[pl.ds(c, res, stride=per_dev), :].astype(jnp.bfloat16)
        rc = stage_b[pl.ds(c, res, stride=per_dev), :].astype(jnp.bfloat16)
        sums.append(dot_nt(lc, rc))
    forward(left_copies, lrecv, l_send, l_recv)
    for c in range(per_dev):
        z = sums[c]
        for p in range(P_):
            got = chunk_swap(
                [z[(p * nch + a) * G : (p * nch + a + 1) * G] for a in range(nch)], cols
            )
            for q in range(Q_):
                stage_a[pl.ds((p * Q_ + q) * unit + c, G, stride=per_dev), :] = got[q]
    for n in range(D_):
        zsend[n] = stage_a[n * unit : (n + 1) * unit, :].astype(jnp.bfloat16)
    zrecv[me] = zsend[me]
    sum_copies = exchange(lambda n: zsend.at[n], zrecv, z_send, z_recv)

    for c in left_copies[P_ - 1 :] + right_copies:
        c.wait_recv()
    total = D_ * half
    for n in range(D_):
        stage_a[n * half : (n + 1) * half, :] = lrecv[n].astype(jnp.float32)
        stage_b[n * half : (n + 1) * half, :] = rrecv[n].astype(jnp.float32)
    seq_all = D_ * seqs
    r_all = jnp.concatenate(
        [stage_b[pl.ds(g, seq_all, stride=SUB), :] for g in range(SUB)], axis=1
    ).astype(jnp.bfloat16)
    for g in range(G):
        lg = stage_a[pl.ds(g, seq_all, stride=SUB), :].T.astype(jnp.bfloat16)
        prod = dot_nn(lg, r_all) * (1.0 / seq_all)
        terms = []
        for k in range(SUB):
            part = prod[:, k * LANES : (k + 1) * LANES]
            got = chunk_swap([part[a * fac : (a + 1) * fac] for a in range(nch)], cols)
            terms.extend([x.astype(jnp.bfloat16) for x in got])
        up = dot_nn(w2t[...], jnp.concatenate(terms, axis=0)).T
        for a in range(nch):
            sl = slice(a * cols, (a + 1) * cols)
            upd[g, sl, :] = pair[a * G + g].astype(jnp.float32) + up[sl]

    for c in sum_copies:
        c.wait_recv()
    for n in range(D_):
        stage_a[n * unit : (n + 1) * unit, :] = zrecv[n].astype(jnp.float32)
    for g in range(G):
        sums_g = jnp.concatenate(
            [stage_a[n * unit + g * per_dev : n * unit + (g + 1) * per_dev, :] for n in range(D_)],
            axis=0,
        ).T
        tn = norm_rows(sums_g, tri_gain[...]).astype(jnp.bfloat16)
        both = upd[g] + gate_f[g] * dot_nn(tn, tri_out[...])
        for a in range(nch):
            i = a * G + g
            sl = slice(a * cols, (a + 1) * cols)
            pair_out[i] = both[sl].astype(jnp.bfloat16)
    for c in bias_copies + tri_copies[0] + tri_copies[1]:
        c.wait_send()
    for c in left_copies + right_copies + sum_copies:
        c.wait_send()


def settle_kernel(one, two, one_out, two_out, one_held, two_held, sems):
    come = [
        pltpu.make_async_copy(one, one_held, sems.at[0]),
        pltpu.make_async_copy(two, two_held, sems.at[1]),
    ]
    go = [
        pltpu.make_async_copy(one_held, one_out, sems.at[2]),
        pltpu.make_async_copy(two_held, two_out, sems.at[3]),
    ]
    for c in come:
        c.start()
    for c, d in zip(come, go):
        c.wait()
        d.start()
    for d in go:
        d.wait()


def kernel_fits(P_, Q_, args):
    feat, pair, head_w, prod_w = args[0], args[3], args[10], args[12]
    rows, cols, cz = pair.shape
    seqs, res, width = feat.shape
    heads = head_w.shape[1]
    fac = prod_w.shape[1] // 2
    nch = LANES // cols
    return (
        res == LANES
        and cz == LANES
        and rows == cols
        and fac == cols
        and nch == P_
        and nch == Q_
        and rows == nch * SUB
        and cz == P_ * Q_ * SUB
        and heads == SUB
        and width % LANES == 0
        and LANES % (width // heads) == 0
        and D_rows(P_, Q_, seqs) <= fac * fac
    )


def D_rows(P_, Q_, seqs):
    return P_ * Q_ * seqs * SUB


def fused(*args):
    P_ = lax.axis_size("dap")
    B_ = lax.axis_size("branch")
    K_ = lax.axis_size("chan")
    Q_ = B_ * K_
    D_ = P_ * Q_
    if not kernel_fits(P_, Q_, args):
        return shards(*args)
    (feat, tokens, amask, pair, pmask, table, focus_gain, entry, exit_w, pair_gain, head_w) = args[:11]
    (product_gain, prod_w, outer_w, tri_w, tri_gain, tri_out) = args[11:]
    rows, cols, cz = pair.shape
    seqs, res, width = feat.shape
    heads = head_w.shape[1]
    fac = prod_w.shape[1] // 2
    nch = LANES // cols
    G = rows // nch
    per = LANES // (width // heads)
    operands = (
        feat,
        tokens,
        amask,
        pair,
        pmask,
        table,
        focus_gain[None, :],
        entry,
        exit_w,
        pair_gain[None, :],
        head_w.T,
        product_gain[None, :],
        prod_w.T,
        outer_w,
        tri_w,
        tri_gain[None, :],
        tri_out,
    )
    order = (3, 9, 10, 14, 4, 0, 1, 5, 6, 7, 13, 12, 2, 8, 11, 15, 16)
    per_dev = cz // D_
    unit = G * per_dev
    half = seqs * SUB
    f32, bf16 = jnp.float32, jnp.bfloat16
    vm = pltpu.VMEM
    dma = pltpu.SemaphoreType.DMA
    results = pl.pallas_call(
        functools.partial(staged_kernel, (P_, B_, K_), order),
        out_shape=(
            jax.ShapeDtypeStruct(feat.shape, bf16),
            jax.ShapeDtypeStruct(pair.shape, bf16),
        ),
        in_specs=[pl.BlockSpec(memory_space=pltpu.HBM)] * len(operands),
        out_specs=(pl.BlockSpec(memory_space=vm), pl.BlockSpec(memory_space=vm)),
        scratch_shapes=[
            vm((rows * cols, cz), bf16),
            vm((G * heads, LANES), f32),
            vm((D_, G * heads, LANES), f32),
            vm((2, D_, unit, LANES), bf16),
            vm((2, D_, unit, LANES), bf16),
            vm((P_, half, LANES), bf16),
            vm((Q_, half, LANES), bf16),
            vm((D_, half, LANES), bf16),
            vm((D_, half, LANES), bf16),
            vm((D_, unit, LANES), bf16),
            vm((D_, unit, LANES), bf16),
            vm((fac * fac, LANES), f32),
            vm((fac * fac, LANES), f32),
            vm((heads * res, LANES), f32),
            vm((seqs, res, width), f32),
            vm((seqs, width // LANES, per * res, LANES), bf16),
            vm((seqs, res, 2 * width), bf16),
            vm((seqs, res, width), f32),
            vm((seqs * res, width), f32),
            vm((cz, fac * fac), bf16),
            vm((G, LANES, LANES), f32),
            vm((LANES, width), f32),
            vm((nch * width, nch * fac), bf16),
            vm((G, LANES, cz), f32),
            dma((D_,)),
            dma((D_,)),
            dma((2, D_)),
            dma((2, D_)),
            dma((D_,)),
            dma((D_,)),
            dma((D_,)),
            dma((D_,)),
            dma((D_,)),
            dma((D_,)),
        ]
        + [vm(x.shape, x.dtype) for x in operands]
        + [dma((len(operands),))],
        compiler_params=pltpu.CompilerParams(collective_id=0, has_side_effects=True),
    )(*operands)
    return pl.pallas_call(
        settle_kernel,
        out_shape=tuple(jax.ShapeDtypeStruct(x.shape, x.dtype) for x in results),
        in_specs=[pl.BlockSpec(memory_space=pltpu.HBM)] * 2,
        out_specs=(pl.BlockSpec(memory_space=pltpu.HBM),) * 2,
        scratch_shapes=[vm(x.shape, x.dtype) for x in results] + [dma((4,))],
    )(*results)


def solution(mesh):
    in_specs = (
        P(("groups", "dap", "branch", "chan"), None, None),
        P(("groups", "dap", "branch", "chan"), None),
        P(("groups", "dap", "branch", "chan"), None),
        P(("groups", "dap"), ("branch", "chan"), None),
        P(("groups", "dap"), ("branch", "chan")),
        P(),
        P(),
        P(),
        P(),
        P(),
        P(),
        P(),
        P(),
        P(),
        P(),
        P(),
        P(),
    )
    out_specs = (
        P(("groups", "dap", "branch", "chan"), None, None),
        P(("groups", "dap"), ("branch", "chan"), None),
    )
    return jax.shard_map(fused, mesh=mesh, in_specs=in_specs, out_specs=out_specs, check_vma=False)
```

profile of v0, /device:TPU:1, one launch (start us, length us, event | category | flops | bytes accessed | tf_op | source)
XLA Modules:
  0.0 37.4 jit_solution(16834779166671024033)
XLA Ops:
  0.6 35.0 %shard_map.176 = (bf16[4,128,256]{2,1,0:T(8,128)(2,1)}, bf16[32,32,128]{2,1,0:T(8,128)(2,1)}) custom-call(bf16[4,128,256]{2,1,0:T(8,128)(2,1)} %refs_0_.1, s32[4,128]{1,0:T(4,128)} %refs_1_.1, s32[4,128]{1,0:T(4,128)} %refs_2_.1, bf16[32,32,128]{2,1,0:T(8,128)(2,1)} %refs_3_.1, s32[32,32]{1,0:T(8,128)} %refs_4_.1, bf16[23,256]{1,0:T(8,128)(2,1)} %refs_5_.1, ...), custom_call_target="tpu_custom_call" | custom-call | tf_op jit(solution)/shard_map/pallas_call | solution.py:740
  35.6 1.8 %shard_map.177 = (bf16[4,128,256]{2,1,0:T(8,128)(2,1)}, bf16[32,32,128]{2,1,0:T(8,128)(2,1)}) custom-call(bf16[4,128,256]{2,1,0:T(8,128)(2,1)} %get-tuple-element.4.one, bf16[32,32,128]{2,1,0:T(8,128)(2,1)} %get-tuple-element.5.two), custom_call_target="tpu_custom_call" | custom-call | tf_op jit(solution)/shard_map/pallas_call | solution.py:788
where the time goes:
time: 37.6 us; the launch traced here: 37.4 us
  Pallas kernels  36.8 us (98%)
  between operations  0.65 us (2%)
    pallas_call x1, Pallas kernels, fused(): pl.pallas_call(functools.partial(staged_kernel, (P_, B_, K_), order), out...  35 us
    pallas_call x1, Pallas kernels, fused(): pl.pallas_call(settle_kernel, out_shape=tuple((jax.ShapeDtypeStruct(x.sha...  1.77 us

commit v1 on v0

--- a/solution.py
+++ b/solution.py
@@ -330,6 +330,8 @@
     normed,
     w2t,
     upd,
+    rblk,
+    obuf,
     table_f,
     left_w,
     gate_f,
@@ -357,15 +359,15 @@
     nch = LANES // cols
     G = rows // nch
     mp = lax.axis_index("dap")
-    mq = lax.axis_index("branch") * K_ + lax.axis_index("chan")
+    mb = lax.axis_index("branch")
+    mk = lax.axis_index("chan")
+    mq = mb * K_ + mk
     me = mp * Q_ + mq
 
-    def where_is(p, q):
-        return {"dap": p, "branch": q // K_, "chan": q % K_}
-
     def peer(off):
-        n = lax.rem(me + off, D_)
-        return n, where_is(n // Q_, n % Q_)
+        dp, db, dk = off // Q_, (off // K_) % B_, off % K_
+        p, b, k = mp ^ dp, mb ^ db, mk ^ dk
+        return p, b * K_ + k, {"dap": p, "branch": b, "chan": k}
 
     def remote(src, dst, ss, rs, dev):
         return pltpu.make_async_remote_copy(
@@ -377,51 +379,39 @@
             device_id_type=pl.DeviceIdType.MESH,
         )
 
-    def exchange(send, recv, ss, rs):
+    def exchange(send, recv, ss, rs, offs):
         copies = []
-        for off in range(1, D_):
-            n, dev = peer(off)
-            c = remote(send(n), recv.at[me], ss.at[off], rs.at[off], dev)
+        for off in offs:
+            p, q, dev = peer(off)
+            c = remote(send(p, q), recv.at[me], ss.at[off], rs.at[off], dev)
             c.start()
             copies.append(c)
         return copies
 
-    def spread(send, recv, ss, rs):
-        copies = []
-        for op in range(1, P_):
-            p = lax.rem(mp + op, P_)
-            copies.append(
-                remote(send(p), recv.at[me], ss.at[op * Q_], rs.at[op * Q_], where_is(p, mq))
-            )
-        for oq in range(1, Q_):
-            dev = where_is(mp, lax.rem(mq + oq, Q_))
-            copies.append(remote(send(mp), recv.at[me], ss.at[oq], rs.at[oq], dev))
-        for c in copies:
-            c.start()
-        return copies
-
     def forward(copies, recv, ss, rs):
         for op in range(1, P_):
             copies[op - 1].wait_recv()
-            src = lax.rem(mp + P_ - op, P_) * Q_ + mq
+            src = (mp ^ op) * Q_ + mq
             for oq in range(1, Q_):
                 c = remote(
-                    recv.at[src],
-                    recv.at[src],
-                    ss.at[op * Q_ + oq],
-                    rs.at[op * Q_ + oq],
-                    where_is(mp, lax.rem(mq + oq, Q_)),
+                    recv.at[src], recv.at[src], ss.at[op * Q_ + oq], rs.at[op * Q_ + oq], peer(oq)[2]
                 )
                 c.start()
                 copies.append(c)
 
+    z_offs = [op * Q_ for op in range(1, P_)]
+    q_offs = list(range(1, Q_))
+    all_offs = sorted(range(1, D_), key=lambda off: (-(off // Q_), off % Q_))
+    near_offs = [off for off in all_offs if (off // K_) % B_ == 0]
+    cross_offs = [off for off in all_offs if (off // K_) % B_ == 1]
+
+    begin()
     barrier = pltpu.get_barrier_semaphore()
     for off in range(1, D_):
         pl.semaphore_signal(
-            barrier, inc=1, device_id=peer(off)[1], device_id_type=pl.DeviceIdType.MESH
-        )
-
-    begin()
+            barrier, inc=1, device_id=peer(off)[2], device_id_type=pl.DeviceIdType.MESH
+        )
+
     ready(3, 9)
     pair_f = pair[...].astype(jnp.float32).reshape(rows * cols, cz)
     pn[...] = norm_rows(pair_f, pair_gain[...]).astype(jnp.bfloat16)
@@ -436,7 +426,16 @@
         bsend[g * heads : (g + 1) * heads, :] = dot_nt(head_t[...], pair_rows(g))
     brecv[me] = bsend[...]
     pl.semaphore_wait(barrier, D_ - 1)
-    bias_copies = spread(lambda p: bsend, brecv, b_send, b_recv)
+    bias_z = exchange(lambda p, q: bsend, brecv, b_send, b_recv, z_offs)
+    xoff = K_
+
+    def pass_on(src, slot, index, off):
+        c = remote(src, brecv.at[slot], b_send.at[index], b_recv.at[index], peer(off)[2])
+        c.start()
+        return c
+
+    bias_x = [pass_on(bsend, me, Q_ * P_, xoff)]
+    bias_c = [pass_on(bsend, me, Q_ * P_ + P_, 1)]
 
     per_dev = cz // D_
     unit = G * per_dev
@@ -462,11 +461,27 @@
         trecv[side, me] = tsend[side, me]
         tri_copies.append(
             exchange(
-                lambda n: tsend.at[side, n], trecv.at[side], t_send.at[side], t_recv.at[side]
+                lambda p, q: tsend.at[side, p * Q_ + q],
+                trecv.at[side],
+                t_send.at[side],
+                t_recv.at[side],
+                near_offs,
             )
         )
 
-    forward(bias_copies, brecv, b_send, b_recv)
+    for op in range(1, P_):
+        bias_z[op - 1].wait_recv()
+        slot = (mp ^ op) * Q_ + mq
+        bias_x.append(pass_on(brecv.at[slot], slot, Q_ * P_ + op, xoff))
+        bias_c.append(pass_on(brecv.at[slot], slot, Q_ * P_ + P_ + op, 1))
+    for side in range(2):
+        tri_copies[side] += exchange(
+            lambda p, q: tsend.at[side, p * Q_ + q],
+            trecv.at[side],
+            t_send.at[side],
+            t_recv.at[side],
+            cross_offs,
+        )
 
     ready(0, 1, 2, 5, 6, 7, 8, 11, 12, 13, 15, 16)
     table_f[...] = jnp.zeros_like(table_f)
@@ -501,7 +516,11 @@
         )
         w2t[:, g * LANES : (g + 1) * LANES] = piece.T.astype(jnp.bfloat16)
 
-    for c in bias_copies[P_ - 1 :]:
+    for op in range(P_):
+        bias_x[op].wait_recv()
+        slot = (mp ^ op) * Q_ + (mb ^ 1) * K_ + mk
+        bias_c.append(pass_on(brecv.at[slot], slot, Q_ * P_ + 2 * P_ + op, 1))
+    for c in bias_c:
         c.wait_recv()
     for p in range(P_):
         got = chunk_swap([brecv[p * Q_ + q] for q in range(Q_)], cols)
@@ -531,22 +550,18 @@
         on = norm_rows(out.astype(jnp.float32), product_gain[...])
         on = on.astype(jnp.bfloat16).astype(jnp.float32)
         mcol = jnp.broadcast_to(amask[s : s + 1, :].astype(jnp.float32), (res, res)).T
-        normed[s * res : (s + 1) * res, :] = on * jnp.concatenate([mcol] * groups, axis=1)
-
-    wide = []
-    for a in range(nch):
-        wide.append(
-            jnp.concatenate(
-                [
-                    normed[s * res + p * rows + a * G : s * res + p * rows + (a + 1) * G, :]
-                    for s in range(seqs)
-                    for p in range(P_)
-                ],
-                axis=0,
-            ).astype(jnp.bfloat16)
-        )
+        for b in range(groups):
+            normed[b, s * res : (s + 1) * res, :] = on[:, b * LANES : (b + 1) * LANES] * mcol
+
+    each = seqs * res // nch
+    wide = [
+        normed[b, pl.ds(a, each, stride=nch), :].astype(jnp.bfloat16)
+        for a in range(nch)
+        for b in range(groups)
+    ]
     left = dot_nn(jnp.concatenate(wide, axis=1), left_w[...])
-    right = dot_nt(prod_t[fac:, :], normed[...].astype(jnp.bfloat16))
+    rows_all = jnp.concatenate([normed[b] for b in range(groups)], axis=1).astype(jnp.bfloat16)
+    right = dot_nt(prod_t[fac:, :], rows_all)
     lefts = [
         jnp.concatenate(
             [left[(s * P_ + p) * G : (s * P_ + p + 1) * G] for s in range(seqs)], axis=0
@@ -567,8 +582,8 @@
         rsend[q] = jnp.concatenate([by_seq[s][q] for s in range(seqs)], axis=0).astype(jnp.bfloat16)
     lrecv[me] = lsend[mp]
     rrecv[me] = rsend[mq]
-    left_copies = spread(lambda p: lsend.at[p], lrecv, l_send, l_recv)
-    right_copies = exchange(lambda n: rsend.at[n % Q_], rrecv, o_send, o_recv)
+    left_copies = exchange(lambda p, q: lsend.at[p], lrecv, l_send, l_recv, z_offs + q_offs)
+    right_copies = exchange(lambda p, q: rsend.at[q], rrecv, o_send, o_recv, all_offs)
 
     for g in range(G):
         gate_f[g] = jax.nn.sigmoid(dot_nn(pair_rows(g), tri_w[:, 4 * cz :]))
@@ -603,7 +618,7 @@
     for n in range(D_):
         zsend[n] = stage_a[n * unit : (n + 1) * unit, :].astype(jnp.bfloat16)
     zrecv[me] = zsend[me]
-    sum_copies = exchange(lambda n: zsend.at[n], zrecv, z_send, z_recv)
+    sum_copies = exchange(lambda p, q: zsend.at[p * Q_ + q], zrecv, z_send, z_recv, all_offs)
 
     for c in left_copies[P_ - 1 :] + right_copies:
         c.wait_recv()
@@ -612,21 +627,43 @@
         stage_a[n * half : (n + 1) * half, :] = lrecv[n].astype(jnp.float32)
         stage_b[n * half : (n + 1) * half, :] = rrecv[n].astype(jnp.float32)
     seq_all = D_ * seqs
-    r_all = jnp.concatenate(
-        [stage_b[pl.ds(g, seq_all, stride=SUB), :] for g in range(SUB)], axis=1
+    gh = G // nch
+    lhs = jnp.concatenate(
+        [
+            jnp.concatenate(
+                [stage_a[pl.ds(a * gh + h, seq_all, stride=SUB), :] for a in range(nch)], axis=0
+            ).T
+            for h in range(gh)
+        ],
+        axis=0,
     ).astype(jnp.bfloat16)
-    for g in range(G):
-        lg = stage_a[pl.ds(g, seq_all, stride=SUB), :].T.astype(jnp.bfloat16)
-        prod = dot_nn(lg, r_all) * (1.0 / seq_all)
-        terms = []
-        for k in range(SUB):
-            part = prod[:, k * LANES : (k + 1) * LANES]
-            got = chunk_swap([part[a * fac : (a + 1) * fac] for a in range(nch)], cols)
-            terms.extend([x.astype(jnp.bfloat16) for x in got])
-        up = dot_nn(w2t[...], jnp.concatenate(terms, axis=0)).T
-        for a in range(nch):
-            sl = slice(a * cols, (a + 1) * cols)
-            upd[g, sl, :] = pair[a * G + g].astype(jnp.float32) + up[sl]
+    lane_col = lax.broadcasted_iota(jnp.int32, (seq_all, LANES), 1) // cols
+    keep = [jnp.where(lane_col == a, 1.0, 0.0).astype(jnp.bfloat16) for a in range(nch)]
+    for k in range(SUB):
+        here = stage_b[pl.ds(k, seq_all, stride=SUB), :]
+        turned = [here] + [pltpu.roll(here, r * cols, 1) for r in range(1, nch)]
+        turned = [x.astype(jnp.bfloat16) for x in turned]
+        for d in range(nch):
+            at = (k * nch + d) * LANES
+            for a in range(nch):
+                rblk[a * seq_all : (a + 1) * seq_all, at : at + LANES] = (
+                    turned[(a - d) % nch] * keep[a]
+                )
+    for t in range(fac // 2):
+        prod = dot_nn(lhs, rblk[:, 2 * t * LANES : 2 * (t + 1) * LANES]).astype(jnp.bfloat16)
+        for g in range(G):
+            for e in range(2):
+                obuf[g // 2, (2 * t + e) * fac : (2 * t + e + 1) * fac, (g % 2) * LANES : (g % 2 + 1) * LANES] = prod[
+                    g * fac : (g + 1) * fac, e * LANES : (e + 1) * LANES
+                ]
+    for t in range(G // 2):
+        both = dot_nn(w2t[...], obuf[t]) * (1.0 / seq_all)
+        for e in range(2):
+            g = 2 * t + e
+            up = both[:, e * LANES : (e + 1) * LANES].T
+            for a in range(nch):
+                sl = slice(a * cols, (a + 1) * cols)
+                upd[g, sl, :] = pair[a * G + g].astype(jnp.float32) + up[sl]
 
     for c in sum_copies:
         c.wait_recv()
@@ -643,7 +680,7 @@
             i = a * G + g
             sl = slice(a * cols, (a + 1) * cols)
             pair_out[i] = both[sl].astype(jnp.bfloat16)
-    for c in bias_copies + tri_copies[0] + tri_copies[1]:
+    for c in bias_z + bias_x + bias_c + tri_copies[0] + tri_copies[1]:
         c.wait_send()
     for c in left_copies + right_copies + sum_copies:
         c.wait_send()
@@ -667,7 +704,8 @@
         d.wait()
 
 
-def kernel_fits(P_, Q_, args):
+def kernel_fits(P_, B_, K_, args):
+    Q_ = B_ * K_
     feat, pair, head_w, prod_w = args[0], args[3], args[10], args[12]
     rows, cols, cz = pair.shape
     seqs, res, width = feat.shape
@@ -687,6 +725,8 @@
         and width % LANES == 0
         and LANES % (width // heads) == 0
         and D_rows(P_, Q_, seqs) <= fac * fac
+        and B_ == 2
+        and K_ == 2
     )
 
 
@@ -700,7 +740,7 @@
     K_ = lax.axis_size("chan")
     Q_ = B_ * K_
     D_ = P_ * Q_
-    if not kernel_fits(P_, Q_, args):
+    if not kernel_fits(P_, B_, K_, args):
         return shards(*args)
     (feat, tokens, amask, pair, pmask, table, focus_gain, entry, exit_w, pair_gain, head_w) = args[:11]
     (product_gain, prod_w, outer_w, tri_w, tri_gain, tri_out) = args[11:]
@@ -734,6 +774,7 @@
     per_dev = cz // D_
     unit = G * per_dev
     half = seqs * SUB
+    seq_all = D_ * seqs
     f32, bf16 = jnp.float32, jnp.bfloat16
     vm = pltpu.VMEM
     dma = pltpu.SemaphoreType.DMA
@@ -764,14 +805,16 @@
             vm((seqs, width // LANES, per * res, LANES), bf16),
             vm((seqs, res, 2 * width), bf16),
             vm((seqs, res, width), f32),
-            vm((seqs * res, width), f32),
+            vm((width // LANES, seqs * res, LANES), f32),
             vm((cz, fac * fac), bf16),
             vm((G, LANES, LANES), f32),
+            vm((nch * seq_all, fac * LANES), bf16),
+            vm((G // 2, fac * fac, 2 * LANES), bf16),
             vm((LANES, width), f32),
             vm((nch * width, nch * fac), bf16),
             vm((G, LANES, cz), f32),
-            dma((D_,)),
-            dma((D_,)),
+            dma((Q_ * P_ + 3 * P_,)),
+            dma((Q_ * P_ + 3 * P_,)),
             dma((2, D_)),
             dma((2, D_)),
             dma((D_,)),

time: 37.6 us -> 39.4 us (1.048)
  the two profiles are of different devices: /device:TPU:1 before, /device:TPU:0 now
where the time goes in v1:
time: 39.4 us; the launch traced here: 39.3 us
  Pallas kernels  38.6 us (98%)
  between operations  0.65 us (2%)
    pallas_call x1, Pallas kernels, fused(): pl.pallas_call(functools.partial(staged_kernel, (P_, B_, K_), order), out...  36.9 us
    pallas_call x1, Pallas kernels, fused(): pl.pallas_call(settle_kernel, out_shape=tuple((jax.ShapeDtypeStruct(x.sha...  1.77 us

profile of v1, /device:TPU:0, one launch (start us, length us, event | category | flops | bytes accessed | tf_op | source)
XLA Modules:
  0.0 39.3 jit_solution(15793668485562294027)
XLA Ops:
  0.6 36.9 %shard_map.176 = (bf16[4,128,256]{2,1,0:T(8,128)(2,1)}, bf16[32,32,128]{2,1,0:T(8,128)(2,1)}) custom-call(bf16[4,128,256]{2,1,0:T(8,128)(2,1)} %refs_0_.1, s32[4,128]{1,0:T(4,128)} %refs_1_.1, s32[4,128]{1,0:T(4,128)} %refs_2_.1, bf16[32,32,128]{2,1,0:T(8,128)(2,1)} %refs_3_.1, s32[32,32]{1,0:T(8,128)} %refs_4_.1, bf16[23,256]{1,0:T(8,128)(2,1)} %refs_5_.1, ...), custom_call_target="tpu_custom_call" | custom-call | tf_op jit(solution)/shard_map/pallas_call | solution.py:781
  37.5 1.8 %shard_map.177 = (bf16[4,128,256]{2,1,0:T(8,128)(2,1)}, bf16[32,32,128]{2,1,0:T(8,128)(2,1)}) custom-call(bf16[4,128,256]{2,1,0:T(8,128)(2,1)} %get-tuple-element.4.one, bf16[32,32,128]{2,1,0:T(8,128)(2,1)} %get-tuple-element.5.two), custom_call_target="tpu_custom_call" | custom-call | tf_op jit(solution)/shard_map/pallas_call | solution.py:831

commit v2 on v1

--- a/solution.py
+++ b/solution.py
@@ -236,6 +236,7 @@
 
 LANES = 128
 SUB = 8
+LOG2E = 1.4426950408889634
 
 
 def dot_nn(left, right):
@@ -266,6 +267,22 @@
 def norm_rows(values, gain):
     center = values - jnp.mean(values, axis=-1, keepdims=True)
     spread = jnp.mean(center * center, axis=-1, keepdims=True)
+    return center * lax.rsqrt(spread + 1e-05) * gain
+
+
+def half_sigmoid(values):
+    return 0.5 * jnp.tanh(0.5 * values) + 0.5
+
+
+def wide_stat(parts, ones, width):
+    total = sum(dot_nn(x, ones) for x in parts) * (1.0 / width)
+    return jnp.concatenate([total] * (width // LANES), axis=1)
+
+
+def norm_mxu(values, parts, gain, ones):
+    width = values.shape[1]
+    center = values - wide_stat(parts, ones, width)
+    spread = wide_stat([(center * center).astype(jnp.bfloat16)], ones, width)
     return center * lax.rsqrt(spread + 1e-05) * gain
 
 
@@ -313,7 +330,8 @@
     bsend,
     brecv,
     tsend,
-    trecv,
+    trecv_l,
+    trecv_r,
     lsend,
     rsend,
     lrecv,
@@ -324,8 +342,13 @@
     stage_b,
     bias_full,
     emb,
-    qm,
-    kv,
+    qd,
+    keys,
+    entry_t,
+    vt,
+    rows_n,
+    att_t,
+    mask_c,
     gates,
     normed,
     w2t,
@@ -336,7 +359,9 @@
     left_w,
     gate_f,
     b_send,
-    b_recv,
+    b_z,
+    b_x,
+    b_c,
     t_send,
     t_recv,
     o_send,
@@ -344,6 +369,7 @@
     z_send,
     z_recv,
     l_send,
+    l_z,
     l_recv,
 ):
     P_, B_, K_ = sizes
@@ -379,31 +405,22 @@
             device_id_type=pl.DeviceIdType.MESH,
         )
 
+    here_dev = peer(1)[2]
+
+    def sent(ref, sem):
+        remote(ref, ref, sem, sem, here_dev).wait_send()
+
+    def arrived(ref, sem):
+        remote(ref, ref, sem, sem, here_dev).wait_recv()
+
     def exchange(send, recv, ss, rs, offs):
-        copies = []
         for off in offs:
             p, q, dev = peer(off)
-            c = remote(send(p, q), recv.at[me], ss.at[off], rs.at[off], dev)
-            c.start()
-            copies.append(c)
-        return copies
-
-    def forward(copies, recv, ss, rs):
-        for op in range(1, P_):
-            copies[op - 1].wait_recv()
-            src = (mp ^ op) * Q_ + mq
-            for oq in range(1, Q_):
-                c = remote(
-                    recv.at[src], recv.at[src], ss.at[op * Q_ + oq], rs.at[op * Q_ + oq], peer(oq)[2]
-                )
-                c.start()
-                copies.append(c)
+            remote(send(p, q), recv.at[me], ss, rs, dev).start()
 
     z_offs = [op * Q_ for op in range(1, P_)]
     q_offs = list(range(1, Q_))
     all_offs = sorted(range(1, D_), key=lambda off: (-(off // Q_), off % Q_))
-    near_offs = [off for off in all_offs if (off // K_) % B_ == 0]
-    cross_offs = [off for off in all_offs if (off // K_) % B_ == 1]
 
     begin()
     barrier = pltpu.get_barrier_semaphore()
@@ -413,8 +430,11 @@
         )
 
     ready(3, 9)
-    pair_f = pair[...].astype(jnp.float32).reshape(rows * cols, cz)
-    pn[...] = norm_rows(pair_f, pair_gain[...]).astype(jnp.bfloat16)
+    pair_h = pair[...].reshape(rows * cols, cz)
+    ones_z = jnp.ones((cz, LANES), jnp.bfloat16)
+    pn[...] = norm_mxu(pair_h.astype(jnp.float32), [pair_h], pair_gain[...], ones_z).astype(
+        jnp.bfloat16
+    )
 
     def pair_rows(g):
         return jnp.concatenate(
@@ -423,92 +443,142 @@
 
     ready(10)
     for g in range(G):
-        bsend[g * heads : (g + 1) * heads, :] = dot_nt(head_t[...], pair_rows(g))
+        stage_b[g * heads : (g + 1) * heads, :] = dot_nt(head_t[...], pair_rows(g)) * LOG2E
+    for b in range(groups):
+        pieces = []
+        for h in range(per):
+            by_head = stage_b[pl.ds(b * per + h, G, stride=heads), :]
+            for a in range(nch):
+                pieces.append(pltpu.roll(by_head, LANES - a * cols, 1) if a else by_head)
+        bsend[b * cols : (b + 1) * cols, :] = jnp.concatenate(pieces, axis=0).T[:cols]
     brecv[me] = bsend[...]
     pl.semaphore_wait(barrier, D_ - 1)
-    bias_z = exchange(lambda p, q: bsend, brecv, b_send, b_recv, z_offs)
+    for op in range(1, P_):
+        p, q, dev = peer(op * Q_)
+        remote(bsend, brecv.at[me], b_send, b_z.at[op], dev).start()
     xoff = K_
 
-    def pass_on(src, slot, index, off):
-        c = remote(src, brecv.at[slot], b_send.at[index], b_recv.at[index], peer(off)[2])
-        c.start()
-        return c
-
-    bias_x = [pass_on(bsend, me, Q_ * P_, xoff)]
-    bias_c = [pass_on(bsend, me, Q_ * P_ + P_, 1)]
-
-    per_dev = cz // D_
+    def pass_on(src, slot, sem, off):
+        remote(src, brecv.at[slot], b_send, sem, peer(off)[2]).start()
+
+    pass_on(bsend, me, b_x.at[0], xoff)
+    pass_on(bsend, me, b_c, 1)
+    half_p = P_ // 2
+    owners = half_p * Q_
+    per_dev = cz // owners
     unit = G * per_dev
+    mine = (mp % half_p) * Q_ + mq
     ready(4, 14)
     mrows = jnp.concatenate(
         [pmask[a * G : (a + 1) * G, :].astype(jnp.float32) for a in range(nch)], axis=1
     )
-    tri_copies = []
-    for side in range(2):
+    trecv = (trecv_l, trecv_r)
+
+    def tri_factor(side):
         at = 2 * side * cz
         tri_t = tri_w[:, at : at + 2 * cz].astype(jnp.float32).T.astype(jnp.bfloat16)
         for t in range(G // 2):
             block = jnp.concatenate([pair_rows(2 * t), pair_rows(2 * t + 1)], axis=0)
             lin = dot_nt(tri_t, block)
             mrow = jnp.concatenate([mrows[2 * t : 2 * t + 1], mrows[2 * t + 1 : 2 * t + 2]], axis=1)
-            val = jax.nn.sigmoid(lin[cz:]) * lin[:cz] * mrow
-            for n in range(D_):
+            val = half_sigmoid(lin[cz:]) * (lin[:cz] * mrow)
+            for n in range(owners):
                 piece = val[n * per_dev : (n + 1) * per_dev]
                 two = jnp.concatenate([piece[:, :LANES], piece[:, LANES:]], axis=0)
                 tsend[side, n, 2 * t * per_dev : 2 * (t + 1) * per_dev, :] = two.astype(
                     jnp.bfloat16
                 )
-        trecv[side, me] = tsend[side, me]
-        tri_copies.append(
-            exchange(
-                lambda p, q: tsend.at[side, p * Q_ + q],
-                trecv.at[side],
+        if side == 0:
+            trecv_l[mine] = tsend[side, mine]
+        else:
+            trecv_r[me] = tsend[side, mine]
+
+    def tri_send(side, offs):
+        for off in offs:
+            p, q, dev = peer(off)
+            slot = mine if side == 0 else me
+            remote(
+                tsend.at[side, (p % half_p) * Q_ + q],
+                trecv[side].at[slot],
                 t_send.at[side],
                 t_recv.at[side],
-                near_offs,
-            )
-        )
-
-    for op in range(1, P_):
-        bias_z[op - 1].wait_recv()
-        slot = (mp ^ op) * Q_ + mq
-        bias_x.append(pass_on(brecv.at[slot], slot, Q_ * P_ + op, xoff))
-        bias_c.append(pass_on(brecv.at[slot], slot, Q_ * P_ + P_ + op, 1))
-    for side in range(2):
-        tri_copies[side] += exchange(
-            lambda p, q: tsend.at[side, p * Q_ + q],
-            trecv.at[side],
-            t_send.at[side],
-            t_recv.at[side],
-            cross_offs,
-        )
+                dev,
+            ).start()
+
+    in_half = [off for off in range(1, D_) if off // Q_ < half_p]
+    far = [off for off in range(1, D_) if off // Q_ >= half_p]
+    own_row = [off for off in in_half if off < Q_]
+    next_row = [off for off in in_half if off >= Q_]
+    same_x = lambda offs: [off for off in offs if (off // K_) % B_ == 0]
+    other_x = lambda offs: [off for off in offs if (off // K_) % B_ == 1]
+    tri_factor(1)
+    tri_send(1, same_x(far))
+    tri_factor(0)
+    tri_send(1, same_x(in_half) + other_x(own_row))
+    tri_send(0, same_x(in_half) + other_x(own_row))
 
     ready(0, 1, 2, 5, 6, 7, 8, 11, 12, 13, 15, 16)
     table_f[...] = jnp.zeros_like(table_f)
     table_f[: table.shape[0], :] = table[...].astype(jnp.float32)
     table_all = table_f[...].astype(jnp.bfloat16)
+    kinds_n = table_f.shape[0]
+    ones_m = jnp.ones((width, LANES), jnp.bfloat16)
+    scale = hw ** (-0.5) * LOG2E
+    for n, at in enumerate((0, 2 * width, 3 * width)):
+        part = entry[:, at : at + width].astype(jnp.float32).T
+        entry_t[n * width : (n + 1) * width, :] = part.astype(jnp.bfloat16)
+    qd[...] = jnp.zeros_like(qd)
+    for s in range(seqs):
+        for h in range(heads):
+            vt[s, h, hw:, :] = jnp.ones((vt.shape[2] - hw, res), jnp.bfloat16)
+    kinds = lax.broadcasted_iota(jnp.int32, (kinds_n, res), 0)
+    hot = jnp.concatenate(
+        [jnp.where(kinds == tokens[s : s + 1, :], 1.0, 0.0) for s in range(seqs)], axis=1
+    ).astype(jnp.float32)
+    here = feat[...].astype(jnp.float32).reshape(seqs * res, width)
+    here = here + dot_nn(hot.T.astype(jnp.bfloat16), table_all)
+    emb[...] = here
+    high = here.astype(jnp.bfloat16)
+    low = (here - high.astype(jnp.float32)).astype(jnp.bfloat16)
+    rows_n[...] = norm_mxu(here, [high, low], focus_gain[...], ones_m).astype(jnp.bfloat16)
+    keys[...] = dot_nn(rows_n[...], entry[:, width : 2 * width]).astype(jnp.bfloat16)
+    for u in range(seqs // 2):
+        two = rows_n[2 * u * res : 2 * (u + 1) * res, :]
+        for n in range(3):
+            turned = dot_nt(entry_t[n * width : (n + 1) * width, :], two)
+            for v in range(2):
+                s = 2 * u + v
+                here = turned[:, v * res : (v + 1) * res]
+                if n == 2:
+                    gates[s] = half_sigmoid(here)
+                    continue
+                for h in range(heads):
+                    b, e = h // per, h % per
+                    part = here[h * hw : (h + 1) * hw]
+                    if n == 0:
+                        qd[s, b, e * hw : (e + 1) * hw, e * res : (e + 1) * res] = (
+                            part * scale
+                        ).astype(jnp.bfloat16)
+                    else:
+                        vt[s, h, :hw, :] = part.astype(jnp.bfloat16)
+
+    for op in range(1, P_):
+        arrived(bsend, b_z.at[op])
+        slot = (mp ^ op) * Q_ + mq
+        pass_on(brecv.at[slot], slot, b_x.at[op], xoff)
+        pass_on(brecv.at[slot], slot, b_c, 1)
+    tri_send(1, other_x(far))
+    tri_send(1, other_x(next_row))
+    tri_send(0, other_x(next_row))
+
     four = jnp.concatenate([prod_t[:fac, :].astype(jnp.float32)] * nch, axis=0).T
     lane_fac = lax.broadcasted_iota(jnp.int32, four.shape, 1) // fac
     for a in range(nch):
         left_w[a * width : (a + 1) * width, :] = jnp.where(lane_fac == a, four, 0.0).astype(
             jnp.bfloat16
         )
-    lane_head = lax.broadcasted_iota(jnp.int32, (res, LANES), 1) // hw
-    for s in range(seqs):
-        kinds = lax.broadcasted_iota(jnp.int32, (LANES, res), 0)
-        hot = jnp.where(kinds == tokens[s : s + 1, :], 1.0, 0.0).astype(jnp.float32)
-        here = feat[s].astype(jnp.float32) + dot_nn(hot.T.astype(jnp.bfloat16), table_all)
-        emb[s] = here
-        proj = dot_nn(norm_rows(here, focus_gain[...]).astype(jnp.bfloat16), entry[...])
-        for b in range(groups):
-            qb = proj[:, b * LANES : (b + 1) * LANES]
-            for h in range(per):
-                qm[s, b, h * res : (h + 1) * res, :] = jnp.where(
-                    lane_head == h, qb, 0.0
-                ).astype(jnp.bfloat16)
-        kv[s] = proj[:, width : 3 * width].astype(jnp.bfloat16)
-        gates[s] = jax.nn.sigmoid(proj[:, 3 * width :])
-
+    for g in range(G):
+        gate_f[g] = half_sigmoid(dot_nn(pair_rows(g), tri_w[:, 4 * cz :]))
     stage_a[...] = outer_w[...].astype(jnp.float32)
     for g in range(SUB):
         piece = jnp.concatenate(
@@ -517,41 +587,41 @@
         w2t[:, g * LANES : (g + 1) * LANES] = piece.T.astype(jnp.bfloat16)
 
     for op in range(P_):
-        bias_x[op].wait_recv()
+        arrived(bsend, b_x.at[op])
         slot = (mp ^ op) * Q_ + (mb ^ 1) * K_ + mk
-        bias_c.append(pass_on(brecv.at[slot], slot, Q_ * P_ + 2 * P_ + op, 1))
-    for c in bias_c:
-        c.wait_recv()
-    for p in range(P_):
-        got = chunk_swap([brecv[p * Q_ + q] for q in range(Q_)], cols)
-        for a in range(nch):
-            stage_a[(p * nch + a) * G * heads : (p * nch + a + 1) * G * heads, :] = got[a]
-    for h in range(heads):
-        bias_full[h * res : (h + 1) * res, :] = stage_a[pl.ds(h, res, stride=heads), :]
-
-    scale = hw ** (-0.5)
+        pass_on(brecv.at[slot], slot, b_c, 1)
+    arrived(brecv.at[: 2 * P_], b_c)
+    for q in range(Q_):
+        for b in range(groups):
+            got = chunk_swap(
+                [brecv[p * Q_ + q, b * cols : (b + 1) * cols, :] for p in range(P_)], cols
+            )
+            for h in range(per):
+                bias_full[b, q * cols : (q + 1) * cols, h * res : (h + 1) * res] = got[h]
+
     for s in range(seqs):
-        mask_row = (amask[s : s + 1, :].astype(jnp.float32) - 1.0) * 1000000000.0
-        gated = []
-        for b in range(groups):
-            key = kv[s, :, b * LANES : (b + 1) * LANES]
-            val = kv[s, :, width + b * LANES : width + (b + 1) * LANES]
-            sc = dot_nt(qm[s, b], key) * scale
-            sc = sc + bias_full[b * per * res : (b + 1) * per * res, :] + mask_row
-            ex = jnp.exp(sc - jnp.max(sc, axis=1, keepdims=True))
-            wt = (ex / jnp.sum(ex, axis=1, keepdims=True)).astype(jnp.bfloat16)
-            av = dot_nn(wt, val)
-            att = av[:res]
-            for h in range(1, per):
-                att = jnp.where(lane_head == h, av[h * res : (h + 1) * res], att)
-            gated.append((att * gates[s, :, b * LANES : (b + 1) * LANES]).astype(jnp.bfloat16))
-        out = (emb[s] + dot_nn(jnp.concatenate(gated, axis=1), exit_w[...])).astype(jnp.bfloat16)
-        align_out[s] = out
-        on = norm_rows(out.astype(jnp.float32), product_gain[...])
-        on = on.astype(jnp.bfloat16).astype(jnp.float32)
         mcol = jnp.broadcast_to(amask[s : s + 1, :].astype(jnp.float32), (res, res)).T
-        for b in range(groups):
-            normed[b, s * res : (s + 1) * res, :] = on[:, b * LANES : (b + 1) * LANES] * mcol
+        mask_add = (mcol - 1.0) * (1000000000.0 * LOG2E)
+        for h in range(heads):
+            b, e = h // per, h % per
+            sl = slice(e * res, (e + 1) * res)
+            sc = dot_nn(
+                keys[s * res : (s + 1) * res, b * LANES : (b + 1) * LANES], qd[s, b, :, sl]
+            )
+            sc = (sc + bias_full[b, :, sl]) + mask_add
+            ex = jnp.exp2(sc - jnp.max(sc, axis=0, keepdims=True)).astype(jnp.bfloat16)
+            av = dot_nn(vt[s, h], ex)
+            att_t[h * hw : (h + 1) * hw, s * res : (s + 1) * res] = (
+                av[:hw] * (1.0 / av[hw : hw + 1]) * gates[s, h * hw : (h + 1) * hw, :]
+            )
+        mask_c[s * res : (s + 1) * res, :] = mcol
+    attended = att_t[...].T.astype(jnp.bfloat16)
+    out = (emb[...] + dot_nn(attended, exit_w[...])).astype(jnp.bfloat16)
+    align_out[...] = out.reshape(seqs, res, width)
+    on = norm_mxu(out.astype(jnp.float32), [out], product_gain[...], ones_m)
+    on = on.astype(jnp.bfloat16).astype(jnp.float32)
+    for b in range(groups):
+        normed[b] = on[:, b * LANES : (b + 1) * LANES] * mask_c[...]
 
     each = seqs * res // nch
     wide = [
@@ -582,46 +652,48 @@
         rsend[q] = jnp.concatenate([by_seq[s][q] for s in range(seqs)], axis=0).astype(jnp.bfloat16)
     lrecv[me] = lsend[mp]
     rrecv[me] = rsend[mq]
-    left_copies = exchange(lambda p, q: lsend.at[p], lrecv, l_send, l_recv, z_offs + q_offs)
-    right_copies = exchange(lambda p, q: rsend.at[q], rrecv, o_send, o_recv, all_offs)
-
-    for g in range(G):
-        gate_f[g] = jax.nn.sigmoid(dot_nn(pair_rows(g), tri_w[:, 4 * cz :]))
+    for op in range(1, P_):
+        p, q, dev = peer(op * Q_)
+        remote(lsend.at[p], lrecv.at[me], l_send, l_z.at[op], dev).start()
+    exchange(lambda p, q: lsend.at[mp], lrecv, l_send, l_recv, q_offs)
+    exchange(lambda p, q: rsend.at[q], rrecv, o_send, o_recv, all_offs)
 
     for side, stage in enumerate((stage_a, stage_b)):
-        for c in tri_copies[side]:
-            c.wait_recv()
-        for p in range(P_):
+        arrived(trecv[side].at[: (owners if side == 0 else D_) - 1], t_recv.at[side])
+        for p in range(half_p if side == 0 else P_):
             got = chunk_swap(
-                [
-                    trecv[side, p * Q_ + q].astype(jnp.float32)
-                    for q in range(Q_)
-                ],
+                [trecv[side][p * Q_ + q].astype(jnp.float32) for q in range(Q_)],
                 cols,
             )
             for a in range(nch):
                 stage[(p * nch + a) * unit : (p * nch + a + 1) * unit, :] = got[a]
     sums = []
     for c in range(per_dev):
-        lc = stage_a[pl.ds(c, res, stride=per_dev), :].astype(jnp.bfloat16)
+        lc = stage_a[pl.ds(c, half_p * rows, stride=per_dev), :].astype(jnp.bfloat16)
         rc = stage_b[pl.ds(c, res, stride=per_dev), :].astype(jnp.bfloat16)
         sums.append(dot_nt(lc, rc))
-    forward(left_copies, lrecv, l_send, l_recv)
+    for op in range(1, P_):
+        arrived(lsend.at[0], l_z.at[op])
+        slot = (mp ^ op) * Q_ + mq
+        for off in q_offs:
+            remote(lrecv.at[slot], lrecv.at[slot], l_send, l_recv, peer(off)[2]).start()
     for c in range(per_dev):
         z = sums[c]
-        for p in range(P_):
+        for p in range(half_p):
             got = chunk_swap(
                 [z[(p * nch + a) * G : (p * nch + a + 1) * G] for a in range(nch)], cols
             )
             for q in range(Q_):
                 stage_a[pl.ds((p * Q_ + q) * unit + c, G, stride=per_dev), :] = got[q]
-    for n in range(D_):
+    for n in range(owners):
         zsend[n] = stage_a[n * unit : (n + 1) * unit, :].astype(jnp.bfloat16)
-    zrecv[me] = zsend[me]
-    sum_copies = exchange(lambda p, q: zsend.at[p * Q_ + q], zrecv, z_send, z_recv, all_offs)
-
-    for c in left_copies[P_ - 1 :] + right_copies:
-        c.wait_recv()
+    zrecv[mine] = zsend[mine]
+    for off in sorted(in_half, reverse=True):
+        p, q, dev = peer(off)
+        remote(zsend.at[(p % half_p) * Q_ + q], zrecv.at[mine], z_send, z_recv, dev).start()
+
+    arrived(lrecv.at[: P_ * (Q_ - 1)], l_recv)
+    arrived(rrecv.at[: D_ - 1], o_recv)
     total = D_ * half
     for n in range(D_):
         stage_a[n * half : (n + 1) * half, :] = lrecv[n].astype(jnp.float32)
@@ -665,13 +737,20 @@
                 sl = slice(a * cols, (a + 1) * cols)
                 upd[g, sl, :] = pair[a * G + g].astype(jnp.float32) + up[sl]
 
-    for c in sum_copies:
-        c.wait_recv()
-    for n in range(D_):
+    sent(brecv.at[: D_ - 1], b_send)
+    sent(trecv_l.at[: owners - 1], t_send.at[0])
+    sent(trecv_r.at[: D_ - 1], t_send.at[1])
+    sent(lrecv.at[: D_ - 1], l_send)
+    sent(rrecv.at[: D_ - 1], o_send)
+    arrived(zrecv.at[: owners - 1], z_recv)
+    for n in range(owners):
         stage_a[n * unit : (n + 1) * unit, :] = zrecv[n].astype(jnp.float32)
     for g in range(G):
         sums_g = jnp.concatenate(
-            [stage_a[n * unit + g * per_dev : n * unit + (g + 1) * per_dev, :] for n in range(D_)],
+            [
+                stage_a[n * unit + g * per_dev : n * unit + (g + 1) * per_dev, :]
+                for n in range(owners)
+            ],
             axis=0,
         ).T
         tn = norm_rows(sums_g, tri_gain[...]).astype(jnp.bfloat16)
@@ -680,10 +759,7 @@
             i = a * G + g
             sl = slice(a * cols, (a + 1) * cols)
             pair_out[i] = both[sl].astype(jnp.bfloat16)
-    for c in bias_z + bias_x + bias_c + tri_copies[0] + tri_copies[1]:
-        c.wait_send()
-    for c in left_copies + right_copies + sum_copies:
-        c.wait_send()
+    sent(zrecv.at[: owners - 1], z_send)
 
 
 def settle_kernel(one, two, one_out, two_out, one_held, two_held, sems):
@@ -723,7 +799,7 @@
         and cz == P_ * Q_ * SUB
         and heads == SUB
         and width % LANES == 0
-        and LANES % (width // heads) == 0
+        and width // heads == cols
         and D_rows(P_, Q_, seqs) <= fac * fac
         and B_ == 2
         and K_ == 2
@@ -771,7 +847,8 @@
         tri_out,
     )
     order = (3, 9, 10, 14, 4, 0, 1, 5, 6, 7, 13, 12, 2, 8, 11, 15, 16)
-    per_dev = cz // D_
+    owners = P_ // 2 * Q_
+    per_dev = cz // owners
     unit = G * per_dev
     half = seqs * SUB
     seq_all = D_ * seqs
@@ -790,39 +867,48 @@
             vm((rows * cols, cz), bf16),
             vm((G * heads, LANES), f32),
             vm((D_, G * heads, LANES), f32),
-            vm((2, D_, unit, LANES), bf16),
-            vm((2, D_, unit, LANES), bf16),
+            vm((2, owners, unit, LANES), bf16),
+            vm((owners, unit, LANES), bf16),
+            vm((D_, unit, LANES), bf16),
             vm((P_, half, LANES), bf16),
             vm((Q_, half, LANES), bf16),
             vm((D_, half, LANES), bf16),
             vm((D_, half, LANES), bf16),
-            vm((D_, unit, LANES), bf16),
-            vm((D_, unit, LANES), bf16),
+            vm((owners, unit, LANES), bf16),
+            vm((owners, unit, LANES), bf16),
             vm((fac * fac, LANES), f32),
-            vm((fac * fac, LANES), f32),
-            vm((heads * res, LANES), f32),
-            vm((seqs, res, width), f32),
-            vm((seqs, width // LANES, per * res, LANES), bf16),
-            vm((seqs, res, 2 * width), bf16),
-            vm((seqs, res, width), f32),
+            vm((res * per_dev, LANES), f32),
+            vm((width // LANES, res, per * res), f32),
+            vm((seqs * res, width), f32),
+            vm((seqs, width // LANES, LANES, per * res), bf16),
+            vm((seqs * res, width), bf16),
+            vm((3 * width, width), bf16),
+            vm((seqs, heads, width // heads + 16, res), bf16),
+            vm((seqs * res, width), bf16),
+            vm((width, seqs * res), f32),
+            vm((seqs * res, LANES), f32),
+            vm((seqs, width, res), f32),
             vm((width // LANES, seqs * res, LANES), f32),
             vm((cz, fac * fac), bf16),
             vm((G, LANES, LANES), f32),
             vm((nch * seq_all, fac * LANES), bf16),
             vm((G // 2, fac * fac, 2 * LANES), bf16),
-            vm((LANES, width), f32),
+            vm((-(-table.shape[0] // 16) * 16, width), f32),
             vm((nch * width, nch * fac), bf16),
             vm((G, LANES, cz), f32),
-            dma((Q_ * P_ + 3 * P_,)),
-            dma((Q_ * P_ + 3 * P_,)),
-            dma((2, D_)),
-            dma((2, D_)),
-            dma((D_,)),
-            dma((D_,)),
-            dma((D_,)),
-            dma((D_,)),
-            dma((D_,)),
-            dma((D_,)),
+            dma,
+            dma((P_,)),
+            dma((P_,)),
+            dma,
+            dma((2,)),
+            dma((2,)),
+            dma,
+            dma,
+            dma,
+            dma,
+            dma,
+            dma((P_,)),
+            dma,
         ]
         + [vm(x.shape, x.dtype) for x in operands]
         + [dma((len(operands),))],

time: 39.4 us -> 34.3 us (0.87)
  Pallas kernels: 38.6 us -> 33.5 us
    pallas_call x1, Pallas kernels: 36.9 us -> 31.7 us  [fused(): pl.pallas_call(functools.partial(staged_kernel, (P_, B_, K_), order), out...]
where the time goes in v2:
time: 34.3 us; the launch traced here: 34.2 us
  Pallas kernels  33.5 us (98%)
  between operations  0.65 us (2%)
    pallas_call x1, Pallas kernels, fused(): pl.pallas_call(functools.partial(staged_kernel, (P_, B_, K_), order), out...  31.7 us
    pallas_call x1, Pallas kernels, fused(): pl.pallas_call(settle_kernel, out_shape=tuple((jax.ShapeDtypeStruct(x.sha...  1.77 us

profile of v2, /device:TPU:0, one launch (start us, length us, event | category | flops | bytes accessed | tf_op | source)
XLA Modules:
  0.0 34.2 jit_solution(15324344703057435397)
XLA Ops:
  0.6 31.7 %shard_map.176 = (bf16[4,128,256]{2,1,0:T(8,128)(2,1)}, bf16[32,32,128]{2,1,0:T(8,128)(2,1)}) custom-call(bf16[4,128,256]{2,1,0:T(8,128)(2,1)} %refs_0_.1, s32[4,128]{1,0:T(4,128)} %refs_1_.1, s32[4,128]{1,0:T(4,128)} %refs_2_.1, bf16[32,32,128]{2,1,0:T(8,128)(2,1)} %refs_3_.1, s32[32,32]{1,0:T(8,128)} %refs_4_.1, bf16[23,256]{1,0:T(8,128)(2,1)} %refs_5_.1, ...), custom_call_target="tpu_custom_call" | custom-call | tf_op jit(solution)/shard_map/pallas_call | solution.py:858
  32.4 1.8 %shard_map.177 = (bf16[4,128,256]{2,1,0:T(8,128)(2,1)}, bf16[32,32,128]{2,1,0:T(8,128)(2,1)}) custom-call(bf16[4,128,256]{2,1,0:T(8,128)(2,1)} %get-tuple-element.4.one, bf16[32,32,128]{2,1,0:T(8,128)(2,1)} %get-tuple-element.5.two), custom_call_target="tpu_custom_call" | custom-call | tf_op jit(solution)/shard_map/pallas_call | solution.py:917

commit v3 on v2

--- a/solution.py
+++ b/solution.py
@@ -340,6 +340,7 @@
     zrecv,
     stage_a,
     stage_b,
+    stage_z,
     bias_full,
     emb,
     qd,
@@ -366,11 +367,14 @@
     t_recv,
     o_send,
     o_recv,
+    o_z,
+    o_f,
     z_send,
     z_recv,
     l_send,
     l_z,
     l_recv,
+    row_in,
 ):
     P_, B_, K_ = sizes
     Q_ = B_ * K_
@@ -422,9 +426,10 @@
     q_offs = list(range(1, Q_))
     all_offs = sorted(range(1, D_), key=lambda off: (-(off // Q_), off % Q_))
 
+    half_p = P_ // 2
     begin()
     barrier = pltpu.get_barrier_semaphore()
-    for off in range(1, D_):
+    for off in z_offs + q_offs:
         pl.semaphore_signal(
             barrier, inc=1, device_id=peer(off)[2], device_id_type=pl.DeviceIdType.MESH
         )
@@ -452,7 +457,11 @@
                 pieces.append(pltpu.roll(by_head, LANES - a * cols, 1) if a else by_head)
         bsend[b * cols : (b + 1) * cols, :] = jnp.concatenate(pieces, axis=0).T[:cols]
     brecv[me] = bsend[...]
-    pl.semaphore_wait(barrier, D_ - 1)
+    pl.semaphore_wait(barrier, P_ + Q_ - 2)
+    for off in z_offs:
+        pl.semaphore_signal(
+            row_in, inc=1, device_id=peer(off)[2], device_id_type=pl.DeviceIdType.MESH
+        )
     for op in range(1, P_):
         p, q, dev = peer(op * Q_)
         remote(bsend, brecv.at[me], b_send, b_z.at[op], dev).start()
@@ -463,9 +472,9 @@
 
     pass_on(bsend, me, b_x.at[0], xoff)
     pass_on(bsend, me, b_c, 1)
-    half_p = P_ // 2
     owners = half_p * Q_
-    per_dev = cz // owners
+    parts_n = 2
+    per_dev = cz // (owners * parts_n)
     unit = G * per_dev
     mine = (mp % half_p) * Q_ + mq
     ready(4, 14)
@@ -483,25 +492,28 @@
             mrow = jnp.concatenate([mrows[2 * t : 2 * t + 1], mrows[2 * t + 1 : 2 * t + 2]], axis=1)
             val = half_sigmoid(lin[cz:]) * (lin[:cz] * mrow)
             for n in range(owners):
-                piece = val[n * per_dev : (n + 1) * per_dev]
-                two = jnp.concatenate([piece[:, :LANES], piece[:, LANES:]], axis=0)
-                tsend[side, n, 2 * t * per_dev : 2 * (t + 1) * per_dev, :] = two.astype(
-                    jnp.bfloat16
-                )
-        if side == 0:
-            trecv_l[mine] = tsend[side, mine]
-        else:
-            trecv_r[me] = tsend[side, mine]
-
-    def tri_send(side, offs):
+                for h in range(parts_n):
+                    at_c = (n * parts_n + h) * per_dev
+                    piece = val[at_c : at_c + per_dev]
+                    two = jnp.concatenate([piece[:, :LANES], piece[:, LANES:]], axis=0)
+                    tsend[side, h, n, 2 * t * per_dev : 2 * (t + 1) * per_dev, :] = two.astype(
+                        jnp.bfloat16
+                    )
+        for h in range(parts_n):
+            if side == 0:
+                trecv_l[h, mine] = tsend[side, h, mine]
+            else:
+                trecv_r[h, me] = tsend[side, h, mine]
+
+    def tri_send(side, h, offs):
         for off in offs:
             p, q, dev = peer(off)
             slot = mine if side == 0 else me
             remote(
-                tsend.at[side, (p % half_p) * Q_ + q],
-                trecv[side].at[slot],
+                tsend.at[side, h, (p % half_p) * Q_ + q],
+                trecv[side].at[h, slot],
                 t_send.at[side],
-                t_recv.at[side],
+                t_recv.at[side, h],
                 dev,
             ).start()
 
@@ -512,10 +524,13 @@
     same_x = lambda offs: [off for off in offs if (off // K_) % B_ == 0]
     other_x = lambda offs: [off for off in offs if (off // K_) % B_ == 1]
     tri_factor(1)
-    tri_send(1, same_x(far))
+    pl.semaphore_wait(row_in, P_ - 1)
+    for h in range(parts_n):
+        tri_send(1, h, same_x(far))
     tri_factor(0)
-    tri_send(1, same_x(in_half) + other_x(own_row))
-    tri_send(0, same_x(in_half) + other_x(own_row))
+    for h in range(parts_n):
+        tri_send(1, h, in_half)
+        tri_send(0, h, in_half)
 
     ready(0, 1, 2, 5, 6, 7, 8, 11, 12, 13, 15, 16)
     table_f[...] = jnp.zeros_like(table_f)
@@ -567,9 +582,8 @@
         slot = (mp ^ op) * Q_ + mq
         pass_on(brecv.at[slot], slot, b_x.at[op], xoff)
         pass_on(brecv.at[slot], slot, b_c, 1)
-    tri_send(1, other_x(far))
-    tri_send(1, other_x(next_row))
-    tri_send(0, other_x(next_row))
+    for h in range(parts_n):
+        tri_send(1, h, other_x(far))
 
     four = jnp.concatenate([prod_t[:fac, :].astype(jnp.float32)] * nch, axis=0).T
     lane_fac = lax.broadcasted_iota(jnp.int32, four.shape, 1) // fac
@@ -656,44 +670,56 @@
         p, q, dev = peer(op * Q_)
         remote(lsend.at[p], lrecv.at[me], l_send, l_z.at[op], dev).start()
     exchange(lambda p, q: lsend.at[mp], lrecv, l_send, l_recv, q_offs)
-    exchange(lambda p, q: rsend.at[q], rrecv, o_send, o_recv, all_offs)
-
-    for side, stage in enumerate((stage_a, stage_b)):
-        arrived(trecv[side].at[: (owners if side == 0 else D_) - 1], t_recv.at[side])
-        for p in range(half_p if side == 0 else P_):
-            got = chunk_swap(
-                [trecv[side][p * Q_ + q].astype(jnp.float32) for q in range(Q_)],
-                cols,
-            )
-            for a in range(nch):
-                stage[(p * nch + a) * unit : (p * nch + a + 1) * unit, :] = got[a]
-    sums = []
-    for c in range(per_dev):
-        lc = stage_a[pl.ds(c, half_p * rows, stride=per_dev), :].astype(jnp.bfloat16)
-        rc = stage_b[pl.ds(c, res, stride=per_dev), :].astype(jnp.bfloat16)
-        sums.append(dot_nt(lc, rc))
-    for op in range(1, P_):
-        arrived(lsend.at[0], l_z.at[op])
-        slot = (mp ^ op) * Q_ + mq
-        for off in q_offs:
-            remote(lrecv.at[slot], lrecv.at[slot], l_send, l_recv, peer(off)[2]).start()
-    for c in range(per_dev):
-        z = sums[c]
-        for p in range(half_p):
-            got = chunk_swap(
-                [z[(p * nch + a) * G : (p * nch + a + 1) * G] for a in range(nch)], cols
-            )
-            for q in range(Q_):
-                stage_a[pl.ds((p * Q_ + q) * unit + c, G, stride=per_dev), :] = got[q]
-    for n in range(owners):
-        zsend[n] = stage_a[n * unit : (n + 1) * unit, :].astype(jnp.bfloat16)
-    zrecv[mine] = zsend[mine]
-    for off in sorted(in_half, reverse=True):
-        p, q, dev = peer(off)
-        remote(zsend.at[(p % half_p) * Q_ + q], zrecv.at[mine], z_send, z_recv, dev).start()
+    cross = [off for off in all_offs if off // Q_ == half_p]
+    exchange(lambda p, q: rsend.at[q], rrecv, o_send, o_z, cross)
+    exchange(lambda p, q: rsend.at[q], rrecv, o_send, o_recv, [off for off in all_offs if off // Q_ < half_p])
+
+    def tri_sums(h):
+        for side, stage in enumerate((stage_a, stage_b)):
+            arrived(trecv[side].at[h, : (owners if side == 0 else D_) - 1], t_recv.at[side, h])
+            for p in range(half_p if side == 0 else P_):
+                got = chunk_swap(
+                    [trecv[side][h, p * Q_ + q].astype(jnp.float32) for q in range(Q_)],
+                    cols,
+                )
+                for a in range(nch):
+                    stage[(p * nch + a) * unit : (p * nch + a + 1) * unit, :] = got[a]
+        for c in range(per_dev):
+            lc = stage_a[pl.ds(c, half_p * rows, stride=per_dev), :].astype(jnp.bfloat16)
+            rc = stage_b[pl.ds(c, res, stride=per_dev), :].astype(jnp.bfloat16)
+            z = dot_nt(lc, rc)
+            for p in range(half_p):
+                got = chunk_swap(
+                    [z[(p * nch + a) * G : (p * nch + a + 1) * G] for a in range(nch)], cols
+                )
+                for q in range(Q_):
+                    stage_z[pl.ds((p * Q_ + q) * unit + c, G, stride=per_dev), :] = got[q]
+        for n in range(owners):
+            zsend[h, n] = stage_z[n * unit : (n + 1) * unit, :].astype(jnp.bfloat16)
+        zrecv[h, mine] = zsend[h, mine]
+        for off in sorted(in_half, reverse=True):
+            p, q, dev = peer(off)
+            remote(
+                zsend.at[h, (p % half_p) * Q_ + q], zrecv.at[h, mine], z_send, z_recv.at[h], dev
+            ).start()
+
+    for h in range(parts_n):
+        tri_sums(h)
+        if h == 0:
+            for op in range(1, P_):
+                arrived(lsend.at[0], l_z.at[op])
+                slot = (mp ^ op) * Q_ + mq
+                for off in q_offs:
+                    remote(
+                        lrecv.at[slot], lrecv.at[slot], l_send, l_recv, peer(off)[2]
+                    ).start()
+            arrived(rrecv.at[:Q_], o_z)
+            theirs = pl.ds((mp ^ half_p) * Q_, Q_)
+            remote(rrecv.at[theirs], rrecv.at[theirs], o_send, o_f, peer(Q_)[2]).start()
 
     arrived(lrecv.at[: P_ * (Q_ - 1)], l_recv)
-    arrived(rrecv.at[: D_ - 1], o_recv)
+    arrived(rrecv.at[: half_p * Q_ - 1], o_recv)
+    arrived(rrecv.at[:Q_], o_f)
     total = D_ * half
     for n in range(D_):
         stage_a[n * half : (n + 1) * half, :] = lrecv[n].astype(jnp.float32)
@@ -721,13 +747,13 @@
                 rblk[a * seq_all : (a + 1) * seq_all, at : at + LANES] = (
                     turned[(a - d) % nch] * keep[a]
                 )
-    for t in range(fac // 2):
-        prod = dot_nn(lhs, rblk[:, 2 * t * LANES : 2 * (t + 1) * LANES]).astype(jnp.bfloat16)
-        for g in range(G):
-            for e in range(2):
-                obuf[g // 2, (2 * t + e) * fac : (2 * t + e + 1) * fac, (g % 2) * LANES : (g % 2 + 1) * LANES] = prod[
-                    g * fac : (g + 1) * fac, e * LANES : (e + 1) * LANES
-                ]
+        for t in range(k * nch // 2, (k + 1) * nch // 2):
+            prod = dot_nn(lhs, rblk[:, 2 * t * LANES : 2 * (t + 1) * LANES]).astype(jnp.bfloat16)
+            for g in range(G):
+                for e in range(2):
+                    obuf[g // 2, (2 * t + e) * fac : (2 * t + e + 1) * fac, (g % 2) * LANES : (g % 2 + 1) * LANES] = prod[
+                        g * fac : (g + 1) * fac, e * LANES : (e + 1) * LANES
+                    ]
     for t in range(G // 2):
         both = dot_nn(w2t[...], obuf[t]) * (1.0 / seq_all)
         for e in range(2):
@@ -738,18 +764,21 @@
                 upd[g, sl, :] = pair[a * G + g].astype(jnp.float32) + up[sl]
 
     sent(brecv.at[: D_ - 1], b_send)
-    sent(trecv_l.at[: owners - 1], t_send.at[0])
-    sent(trecv_r.at[: D_ - 1], t_send.at[1])
+    sent(trecv_l.at[:, : owners - 1], t_send.at[0])
+    sent(trecv_r.at[:, : D_ - 1], t_send.at[1])
     sent(lrecv.at[: D_ - 1], l_send)
     sent(rrecv.at[: D_ - 1], o_send)
-    arrived(zrecv.at[: owners - 1], z_recv)
+    for h in range(parts_n):
+        arrived(zrecv.at[h, : owners - 1], z_recv.at[h])
     for n in range(owners):
-        stage_a[n * unit : (n + 1) * unit, :] = zrecv[n].astype(jnp.float32)
+        for h in range(parts_n):
+            at_c = (n * parts_n + h) * unit
+            stage_a[at_c : at_c + unit, :] = zrecv[h, n].astype(jnp.float32)
     for g in range(G):
         sums_g = jnp.concatenate(
             [
                 stage_a[n * unit + g * per_dev : n * unit + (g + 1) * per_dev, :]
-                for n in range(owners)
+                for n in range(owners * parts_n)
             ],
             axis=0,
         ).T
@@ -759,7 +788,7 @@
             i = a * G + g
             sl = slice(a * cols, (a + 1) * cols)
             pair_out[i] = both[sl].astype(jnp.bfloat16)
-    sent(zrecv.at[: owners - 1], z_send)
+    sent(zrecv.at[:, : owners - 1], z_send)
 
 
 def settle_kernel(one, two, one_out, two_out, one_held, two_held, sems):
@@ -801,6 +830,7 @@
         and width % LANES == 0
         and width // heads == cols
         and D_rows(P_, Q_, seqs) <= fac * fac
+        and P_ == 4
         and B_ == 2
         and K_ == 2
     )
@@ -848,7 +878,8 @@
     )
     order = (3, 9, 10, 14, 4, 0, 1, 5, 6, 7, 13, 12, 2, 8, 11, 15, 16)
     owners = P_ // 2 * Q_
-    per_dev = cz // owners
+    parts_n = 2
+    per_dev = cz // (owners * parts_n)
     unit = G * per_dev
     half = seqs * SUB
     seq_all = D_ * seqs
@@ -867,17 +898,18 @@
             vm((rows * cols, cz), bf16),
             vm((G * heads, LANES), f32),
             vm((D_, G * heads, LANES), f32),
-            vm((2, owners, unit, LANES), bf16),
-            vm((owners, unit, LANES), bf16),
-            vm((D_, unit, LANES), bf16),
+            vm((2, parts_n, owners, unit, LANES), bf16),
+            vm((parts_n, owners, unit, LANES), bf16),
+            vm((parts_n, D_, unit, LANES), bf16),
             vm((P_, half, LANES), bf16),
             vm((Q_, half, LANES), bf16),
             vm((D_, half, LANES), bf16),
             vm((D_, half, LANES), bf16),
-            vm((owners, unit, LANES), bf16),
-            vm((owners, unit, LANES), bf16),
+            vm((parts_n, owners, unit, LANES), bf16),
+            vm((parts_n, owners, unit, LANES), bf16),
             vm((fac * fac, LANES), f32),
-            vm((res * per_dev, LANES), f32),
+            vm((fac * fac, LANES), f32),
+            vm((owners * unit, LANES), f32),
             vm((width // LANES, res, per * res), f32),
             vm((seqs * res, width), f32),
             vm((seqs, width // LANES, LANES, per * res), bf16),
@@ -901,14 +933,17 @@
             dma((P_,)),
             dma,
             dma((2,)),
-            dma((2,)),
+            dma((2, parts_n)),
             dma,
             dma,
             dma,
             dma,
             dma,
+            dma((parts_n,)),
+            dma,
             dma((P_,)),
             dma,
+            pltpu.SemaphoreType.REGULAR,
         ]
         + [vm(x.shape, x.dtype) for x in operands]
         + [dma((len(operands),))],

time: 34.3 us -> 32.2 us (0.939)
  Pallas kernels: 33.5 us -> 31.4 us
    pallas_call x1, Pallas kernels: 31.7 us -> 29.6 us  [fused(): pl.pallas_call(functools.partial(staged_kernel, (P_, B_, K_), order), out...]
where the time goes in v3:
time: 32.2 us; the launch traced here: 32 us
  Pallas kernels  31.4 us (98%)
  between operations  0.65 us (2%)
    pallas_call x1, Pallas kernels, fused(): pl.pallas_call(functools.partial(staged_kernel, (P_, B_, K_), order), out...  29.6 us
    pallas_call x1, Pallas kernels, fused(): pl.pallas_call(settle_kernel, out_shape=tuple((jax.ShapeDtypeStruct(x.sha...  1.77 us

profile of v3, /device:TPU:0, one launch (start us, length us, event | category | flops | bytes accessed | tf_op | source)
XLA Modules:
  0.0 32.0 jit_solution(3508420251331364226)
XLA Ops:
  0.6 29.6 %shard_map.176 = (bf16[4,128,256]{2,1,0:T(8,128)(2,1)}, bf16[32,32,128]{2,1,0:T(8,128)(2,1)}) custom-call(bf16[4,128,256]{2,1,0:T(8,128)(2,1)} %refs_0_.1, s32[4,128]{1,0:T(4,128)} %refs_1_.1, s32[4,128]{1,0:T(4,128)} %refs_2_.1, bf16[32,32,128]{2,1,0:T(8,128)(2,1)} %refs_3_.1, s32[32,32]{1,0:T(8,128)} %refs_4_.1, bf16[23,256]{1,0:T(8,128)(2,1)} %refs_5_.1, ...), custom_call_target="tpu_custom_call" | custom-call | tf_op jit(solution)/shard_map/pallas_call | solution.py:889
  30.2 1.8 %shard_map.177 = (bf16[4,128,256]{2,1,0:T(8,128)(2,1)}, bf16[32,32,128]{2,1,0:T(8,128)(2,1)}) custom-call(bf16[4,128,256]{2,1,0:T(8,128)(2,1)} %get-tuple-element.4.one, bf16[32,32,128]{2,1,0:T(8,128)(2,1)} %get-tuple-element.5.two), custom_call_target="tpu_custom_call" | custom-call | tf_op jit(solution)/shard_map/pallas_call | solution.py:952

commit v4 on v3

--- a/solution.py
+++ b/solution.py
@@ -524,9 +524,11 @@
     same_x = lambda offs: [off for off in offs if (off // K_) % B_ == 0]
     other_x = lambda offs: [off for off in offs if (off // K_) % B_ == 1]
     tri_factor(1)
+    for h in range(parts_n):
+        tri_send(1, h, [off for off in far if off in z_offs])
     pl.semaphore_wait(row_in, P_ - 1)
     for h in range(parts_n):
-        tri_send(1, h, same_x(far))
+        tri_send(1, h, [off for off in same_x(far) if off not in z_offs])
     tri_factor(0)
     for h in range(parts_n):
         tri_send(1, h, in_half)

time: 32.2 us -> 33 us (1.025)
  Pallas kernels: 31.4 us -> 32.2 us
    pallas_call x1, Pallas kernels: 29.6 us -> 30.4 us  [fused(): pl.pallas_call(functools.partial(staged_kernel, (P_, B_, K_), order), out...]
where the time goes in v4:
time: 33 us; the launch traced here: 32.8 us
  Pallas kernels  32.2 us (98%)
  between operations  0.65 us (2%)
    pallas_call x1, Pallas kernels, fused(): pl.pallas_call(functools.partial(staged_kernel, (P_, B_, K_), order), out...  30.4 us
    pallas_call x1, Pallas kernels, fused(): pl.pallas_call(settle_kernel, out_shape=tuple((jax.ShapeDtypeStruct(x.sha...  1.77 us

profile of v4, /device:TPU:0, one launch (start us, length us, event | category | flops | bytes accessed | tf_op | source)
XLA Modules:
  0.0 32.8 jit_solution(3301067029599866402)
XLA Ops:
  0.6 30.4 %shard_map.176 = (bf16[4,128,256]{2,1,0:T(8,128)(2,1)}, bf16[32,32,128]{2,1,0:T(8,128)(2,1)}) custom-call(bf16[4,128,256]{2,1,0:T(8,128)(2,1)} %refs_0_.1, s32[4,128]{1,0:T(4,128)} %refs_1_.1, s32[4,128]{1,0:T(4,128)} %refs_2_.1, bf16[32,32,128]{2,1,0:T(8,128)(2,1)} %refs_3_.1, s32[32,32]{1,0:T(8,128)} %refs_4_.1, bf16[23,256]{1,0:T(8,128)(2,1)} %refs_5_.1, ...), custom_call_target="tpu_custom_call" | custom-call | tf_op jit(solution)/shard_map/pallas_call | solution.py:891
  31.0 1.8 %shard_map.177 = (bf16[4,128,256]{2,1,0:T(8,128)(2,1)}, bf16[32,32,128]{2,1,0:T(8,128)(2,1)}) custom-call(bf16[4,128,256]{2,1,0:T(8,128)(2,1)} %get-tuple-element.4.one, bf16[32,32,128]{2,1,0:T(8,128)(2,1)} %get-tuple-element.5.two), custom_call_target="tpu_custom_call" | custom-call | tf_op jit(solution)/shard_map/pallas_call | solution.py:954
